TPU v7x, 32 devices: a whole 2x2x4 slice. The times are simulated.
32 devices in a mesh: seq: 8 (over z, x), tp: 4 (over y, core).
Axes of the slice: x: 2, y: 2, z: 4, core: 2. Of those that a mesh axis runs over, the one named last changes fastest.
Arguments:
- queries: bfloat16 [4096, 4096], P('seq', 'tp'), may hold values from -6 to 6
- keys: bfloat16 [4096, 4096], P('seq', 'tp'), may hold values from -6 to 6
- values: bfloat16 [4096, 4096], P('seq', 'tp'), may hold values from -6 to 6
- log_decay: float32 [4096, 32], P('seq', 'tp'), may hold values from -1.2 to 0, as said below
- out_weight: bfloat16 [4096, 6144], P('tp', 'seq'), may hold values from -0.09375 to 0.09375
- grad_out: bfloat16 [4096, 6144], P('seq', 'tp'), may hold values from -6 to 6
Outputs:
- grad_queries: bfloat16 [4096, 4096], P('seq', 'tp')
- grad_keys: bfloat16 [4096, 4096], P('seq', 'tp')
- grad_values: bfloat16 [4096, 4096], P('seq', 'tp')
- grad_weight: float32 [6144, 4096], P('seq', 'tp')
Inputs may be any that keep to these rules, and one draw needn't show every extreme that they name: `log_decay`: log decay of each head's state at each token.
All inputs are finite; a program needn't handle non-finite values.
Results may differ from a plain program's by a relative error of at most 0.0029.
Values may be sent and summed in bfloat16 or wider, within the bound.
A program may use at most 192 MiB of HBM per device.

v0:
```python
import jax
import jax.numpy as jnp
from jax import lax
from jax.sharding import PartitionSpec as P

BLOCK = 256


EPS = 1e-06
HIGH = lax.Precision.HIGHEST


def carried_in(value, axis, join, neutral, backward):
    count, mine = (lax.axis_size(axis), lax.axis_index(axis))
    pieces = jax.tree.map(lambda part: lax.all_gather(part, axis), value)
    if backward:
        pieces = jax.tree.map(lambda part: part[::-1], pieces)
        mine = count - 1 - mine
    total = jax.tree.map(
        lambda part, zero: jnp.full_like(part, 0) + jnp.asarray(zero, part.dtype), value, neutral
    )

    def turn(position, total):
        longer = join(total, jax.tree.map(lambda part: part[position], pieces))
        return jax.tree.map(lambda new, old: jnp.where(position < mine, new, old), longer, total)

    return lax.fori_loop(0, count - 1, turn, total)


def chain(earlier, later):
    log_early, state_early = earlier
    log_late, state_late = later
    return (log_early + log_late, jnp.exp(log_late)[:, None, None] * state_early + state_late)


def on_device(queries, keys, values, log_decay, out_weight, grad_out):
    tok_rows = queries.shape[0]
    heads_here = log_decay.shape[1]
    head_size = queries.shape[1] // heads_here
    blocks = tok_rows // BLOCK
    shape4 = (blocks, BLOCK, heads_here, head_size)
    query_b = queries.reshape(shape4)
    key_b = keys.reshape(shape4)
    query_f = queries.astype(jnp.float32).reshape(shape4)
    key_f = keys.astype(jnp.float32).reshape(shape4)
    value_f = values.astype(jnp.float32).reshape(shape4)
    rates = log_decay.reshape(blocks, BLOCK, heads_here)
    cumul = jnp.cumsum(rates, axis=1)
    totals = cumul[:, -1, :]
    running = jnp.cumsum(totals, axis=0)
    before = running - totals
    dev_log = running[-1]
    cumul_t = jnp.transpose(cumul, (0, 2, 1))
    lower = jnp.arange(BLOCK)[:, None] >= jnp.arange(BLOCK)[None, :]
    decay_mat = jnp.where(
        lower[None, None],
        jnp.exp(jnp.minimum(cumul_t[:, :, :, None] - cumul_t[:, :, None, :], 0.0)),
        0.0,
    )
    scores = (
        jnp.einsum("nthd,nshd->nhts", query_b, key_b, preferred_element_type=jnp.float32)
        * decay_mat
    )
    into_end = jnp.exp(totals[:, None, :] - cumul)
    from_start = jnp.exp(cumul)
    block_states = jnp.einsum("nth,nthd,nthe->nhde", into_end, key_f, value_f, precision=HIGH)
    order = jnp.arange(blocks)
    earlier_mask = order[None, :] < order[:, None]
    forward_mix = jnp.where(
        earlier_mask[:, :, None],
        jnp.exp(jnp.minimum(before[:, None, :] - running[None, :, :], 0.0)),
        0.0,
    )
    prefix_local = jnp.einsum("nmh,mhde->nhde", forward_mix, block_states, precision=HIGH)
    dev_state = jnp.einsum(
        "mh,mhde->hde", jnp.exp(dev_log[None, :] - running), block_states, precision=HIGH
    )
    zero_log = jnp.zeros_like(dev_log)
    zero_state = jnp.zeros_like(dev_state)
    state_in = carried_in((dev_log, dev_state), "seq", chain, (zero_log, zero_state), False)[1]
    start_states = prefix_local + jnp.exp(before)[:, :, None, None] * state_in[None]
    attended = jnp.einsum("nhts,nshd->nthd", scores, value_f, precision=HIGH)
    attended = attended + from_start[..., None] * jnp.einsum(
        "nthd,nhde->nthe", query_f, start_states, precision=HIGH
    )
    scale = jnp.sqrt(jnp.mean(attended * attended, axis=-1, keepdims=True) + EPS)
    o_hat = attended / scale
    normed = o_hat.reshape(tok_rows, -1).astype(jnp.bfloat16)
    cotangent = lax.all_gather(grad_out, "tp", axis=1, tiled=True)
    grad_normed = lax.dot_general(
        cotangent,
        lax.all_gather(out_weight, "seq", axis=1, tiled=True),
        (((1,), (1,)), ((), ())),
        preferred_element_type=jnp.float32,
    )
    grad_hat = grad_normed.reshape(shape4)
    grad_att = (grad_hat - o_hat * jnp.mean(grad_hat * o_hat, axis=-1, keepdims=True)) / scale
    grad_mix = jnp.einsum("nthe,nshe->nhts", grad_att, value_f, precision=HIGH) * decay_mat
    grad_q = jnp.einsum("nhts,nshd->nthd", grad_mix, key_f, precision=HIGH)
    grad_q = grad_q + from_start[..., None] * jnp.einsum(
        "nthe,nhde->nthd", grad_att, start_states, precision=HIGH
    )
    block_grads = jnp.einsum("nth,nthd,nthe->nhde", from_start, query_f, grad_att, precision=HIGH)
    later_mask = order[None, :] > order[:, None]
    backward_mix = jnp.where(
        later_mask[:, :, None],
        jnp.exp(jnp.minimum(before[None, :, :] - running[:, None, :], 0.0)),
        0.0,
    )
    suffix_local = jnp.einsum("nmh,mhde->nhde", backward_mix, block_grads, precision=HIGH)
    dev_grad = jnp.einsum("mh,mhde->hde", jnp.exp(before), block_grads, precision=HIGH)
    grad_in = carried_in((dev_log, dev_grad), "seq", chain, (zero_log, zero_state), True)[1]
    end_grads = suffix_local + jnp.exp(dev_log[None, :] - running)[:, :, None, None] * grad_in[None]
    grad_k = jnp.einsum("nhts,nthd->nshd", grad_mix, query_f, precision=HIGH)
    grad_k = grad_k + into_end[..., None] * jnp.einsum(
        "nthe,nhde->nthd", value_f, end_grads, precision=HIGH
    )
    grad_v = jnp.einsum("nhts,nthe->nshe", scores, grad_att, precision=HIGH)
    grad_v = grad_v + into_end[..., None] * jnp.einsum(
        "nthd,nhde->nthe", key_f, end_grads, precision=HIGH
    )
    by_columns = lax.all_to_all(cotangent, "seq", split_axis=1, concat_axis=0, tiled=True)
    grad_weight = lax.dot_general(
        by_columns,
        lax.all_gather(normed, "seq", axis=0, tiled=True),
        (((0,), (0,)), ((), ())),
        preferred_element_type=jnp.float32,
    )
    return (
        grad_q.reshape(tok_rows, -1).astype(jnp.bfloat16),
        grad_k.reshape(tok_rows, -1).astype(jnp.bfloat16),
        grad_v.reshape(tok_rows, -1).astype(jnp.bfloat16),
        grad_weight,
    )


def solution(mesh):
    placed = (
        P("seq", "tp"),
        P("seq", "tp"),
        P("seq", "tp"),
        P("seq", "tp"),
        P("tp", "seq"),
        P("seq", "tp"),
    )
    return jax.shard_map(
        on_device,
        mesh=mesh,
        in_specs=placed,
        out_specs=(P("seq", "tp"), P("seq", "tp"), P("seq", "tp"), P("seq", "tp")),
        check_vma=False,
    )
```

profile of v0, /device:TPU:0, one launch (start us, length us, event | category | flops | bytes accessed | tf_op | source)
XLA Modules:
  0.0 678.1 jit_solution(5137441906326079839)
XLA Ops:
  17.3 4.4 fusion.47
  27.6 22.4 %all-gather.2 = f32[8,1,8]{2,1,0:T(1,128)S(1)} all-gather(f32[1,1,8]{2,1,0:T(1,128)S(1)} %get-tuple-element.278), channel_id=1, replica_groups=mesh['seq'=8,'tp'=4] {'seq'}, dimensions={0}, use_global_device_ids=true | all-gather | bytes 288 | tf_op jit(solution)/shard_map/all_gather | solution.py:15
  50.0 6.3 fusion.49
  60.4 5.3 fusion.6
  65.7 32.3 %all-gather.15.cloned.1.call-done = f32[64,128,128]{2,1,0:T(8,128)} async-done(((f32[8,128,128]{2,1,0:T(8,128)}), f32[64,128,128]{2,1,0:T(8,128)}) %all-gather.15.cloned.1.call-update) | async-done | bytes 4194320 | tf_op jit(solution)/shard_map/all_gather | solution.py:15
  98.0 8.7 %while.28 = (s32[]{:T(128)}, f32[8,128,128]{2,1,0:T(8,128)S(1)}, s32[]{:T(128)}, f32[8,8]{1,0:T(8,128)S(1)}, f32[8,8,128,128]{3,2,1,0:T(8,128)}, /*index=5*/s32[]{:T(128)}, s32[]{:T(128)}) while((s32[]{:T(128)}, f32[8,128,128]{2,1,0:T(8,128)S(1)}, s32[]{:T(128)}, f32[8,8]{1,0:T(8,128)S(1)}, f32[8,8,128,128]{3,2,1,0:T(8,128)}, ...), condition=%wide.region_4.5_spmd.clone, body=%wide.region_3.4_spmd.clone.sunk | while | flops 524292 | bytes 1573073 | solution.py:27
  106.7 4.5 multiply_reduce_fusion.1
  111.2 33.0 %all-gather.9.cloned.1.call-done = bf16[512,6144]{0,1:T(8,128)(2,1)} async-done(((bf16[512,1536]{0,1:T(8,128)(2,1)}), bf16[512,6144]{0,1:T(8,128)(2,1)}) %all-gather.9.cloned.1.call-update) | async-done | bytes 6291472 | tf_op jit(solution)/shard_map/all_gather | solution.py:89
  144.3 178.5 %all-gather.11.cloned.1.call-done = bf16[1024,6144]{1,0:T(8,128)(2,1)} async-done(((bf16[1024,768]{1,0:T(8,128)(2,1)}), bf16[1024,6144]{1,0:T(8,128)(2,1)}) %all-gather.11.cloned.1.call-update) | async-done | bytes 12582928 | tf_op jit(solution)/shard_map/all_gather | solution.py:92
  322.7 11.5 %convolution_bitcast_fusion.1 = f32[64,8,8,128]{3,1,2,0:T(8,128)S(1)} fusion(bf16[512,6144]{0,1:T(8,128)(2,1)} %all-gather.9.cloned.1.call-done, bf16[1024,6144]{1,0:T(8,128)(2,1)} %all-gather.11.cloned.1.call-done), kind=kOutput, calls=%fused_computation.50 | convolution fusion | flops 6442450944 | bytes 20971520 | tf_op jit(solution)/shard_map/dot_general | solution.py:90
  347.5 4.6 fusion.43
  352.1 4.8 all-to-all-start
  362.1 193.0 %all-to-all-done = bf16[512,8,768]{0,2,1:T(8,128)(2,1)} async-done(((bf16[512,8,768]{0,2,1:T(8,128)(2,1)}), bf16[512,8,768]{0,2,1:T(8,128)(2,1)}, u32[]{:S(2)}, u32[]{:S(2)}) %all-to-all-start) | async-done | bytes 6291488 | tf_op jit(solution)/shard_map/all_to_all | solution.py:122
  555.0 8.6 %copy.211 = bf16[8,512,768]{2,1,0:T(8,128)(2,1)} copy(bf16[8,512,768]{1,2,0:T(8,128)(2,1)} %bitcast.34) | data formatting | bytes 12582912 | tf_op jit(solution)/shard_map/all_to_all | solution.py:122
  563.7 3.2 fusion.53
  566.9 3.7 fusion.10
  579.0 6.3 fusion.45
  585.3 8.1 %fusion.8 = f32[2,8,256,128]{3,2,1,0:T(8,128)} fusion(bf16[2,256,8,128]{1,3,2,0:T(8,128)(2,1)S(1)} %copy-done.6, f32[2,8,256,256]{3,2,1,0:T(8,128)} %copy-done.13, f32[2,8,256]{2,1,0:T(8,128)S(1)} %add_bitcast_fusion.1, pred[256,256]{1,0:T(8,128)(4,1)S(1)} %iota_compare_fusion), kind=kOutput, calls=%fused_computation.11 | convolution fusion | flops 1614807040 | bytes 7421952 | tf_op jit(solution)/shard_map/nhts,nthd->nshd/dot_general | solution.py:114
  593.4 9.3 %fusion.4 = f32[2,8,128,256]{2,3,1,0:T(8,128)} fusion(f32[2,256,8,128]{1,3,2,0:T(8,128)S(1)} %get-tuple-element.275, f32[2,8,256,256]{3,2,1,0:T(8,128)S(1)} %copy-done.3, f32[2,8,256]{2,1,0:T(8,128)S(1)} %add_bitcast_fusion.1, pred[256,256]{1,0:T(8,128)(4,1)S(1)} %iota_compare_fusion), kind=kOutput, calls=%fused_computation.9 | convolution fusion | flops 1614807040 | bytes 8470528 | tf_op jit(solution)/shard_map/nhts,nthe->nshe/dot_general | solution.py:118
  602.7 4.7 rev.7
  607.4 8.6 %while.29 = (s32[]{:T(128)}, f32[8,128,128]{2,1,0:T(8,128)S(1)}, s32[]{:T(128)}, f32[8,8]{1,0:T(8,128)S(1)}, f32[8,8,128,128]{3,2,1,0:T(8,128)}, /*index=5*/s32[]{:T(128)}, s32[]{:T(128)}) while((s32[]{:T(128)}, f32[8,128,128]{2,1,0:T(8,128)S(1)}, s32[]{:T(128)}, f32[8,8]{1,0:T(8,128)S(1)}, f32[8,8,128,128]{3,2,1,0:T(8,128)}, ...), condition=%wide.region_8.9_spmd.clone, body=%wide.region_7.8_spmd.clone.sunk | while | flops 524292 | bytes 1573073 | solution.py:27
  616.0 3.4 fusion.13
  624.4 33.4 %all-gather.13.cloned.1.call-done = bf16[4096,1024]{1,0:T(8,128)(2,1)} async-done(((bf16[512,1024]{1,0:T(8,128)(2,1)}), bf16[4096,1024]{1,0:T(8,128)(2,1)}) %all-gather.13.cloned.1.call-update) | async-done | bytes 8388624 | tf_op jit(solution)/shard_map/all_gather | solution.py:125
  657.7 11.0 %convolution_bitcast_fusion = f32[768,1024]{0,1:T(8,128)S(1)} fusion(bf16[4096,1024]{1,0:T(8,128)(2,1)} %all-gather.13.cloned.1.call-done, bf16[4096,768]{1,0:T(8,128)(2,1)} %bitcast.156), kind=kOutput, calls=%fused_computation.49 | convolution fusion | flops 6442450944 | bytes 17825792 | tf_op jit(solution)/shard_map/dot_general | solution.py:123
  (126 shorter events, 70.8 us)
Async XLA Ops:
  7.2 90.8 %all-gather.15.cloned.1.call-start = ((), (), s32[]{:S(2)}) async-start(), calls=%async_computation.4 | async-start | bytes 4718592 | tf_op jit(solution)/shard_map/all_gather | solution.py:15
  11.6 1.9 copy-start.10
  13.5 44.8 %copy-start.8 = (bf16[64,8,8,128]{3,2,1,0:T(8,128)(2,1)}, bf16[64,8,8,128]{3,2,1,0:T(8,128)(2,1)S(1)}, u32[]{:S(2)}) copy-start(bf16[64,8,8,128]{3,2,1,0:T(8,128)(2,1)S(1)} %copy.234) | copy-start | bytes 3145732
  13.5 8.3 %copy-start.16 = (bf16[512,1536]{1,0:T(8,128)(2,1)S(1)}, bf16[512,1536]{1,0:T(8,128)(2,1)}, u32[]{:S(2)}) copy-start(bf16[512,1536]{1,0:T(8,128)(2,1)} %param.15) | copy-start | bytes 4718596
  21.7 122.5 %all-gather.9.cloned.1.call-start = ((), (), s32[]{:S(2)}) async-start(), calls=%async_computation.1 | async-start | bytes 7864320 | tf_op jit(solution)/shard_map/all_gather | solution.py:89
  23.4 1.3 copy-start.18
  23.4 299.3 %all-gather.11.cloned.1.call-start = ((), (), s32[]{:S(2)}) async-start(), calls=%async_computation.2 | async-start | bytes 14155776 | tf_op jit(solution)/shard_map/all_gather | solution.py:92
  24.1 578.5 %all-gather.17.cloned.1.call-start = ((), (), s32[]{:S(2)}) async-start(), calls=%async_computation.5 | async-start | bytes 4718592 | tf_op jit(solution)/shard_map/all_gather | solution.py:15
  27.6 30.8 %copy-start.4 = (bf16[2,256,8,128]{1,3,2,0:T(8,128)(2,1)}, bf16[2,256,8,128]{1,3,2,0:T(8,128)(2,1)S(1)}, u32[]{:S(2)}) copy-start(bf16[2,256,8,128]{1,3,2,0:T(8,128)(2,1)S(1)} %copy.196) | copy-start | bytes 3145732
  58.3 2.0 copy-start.2
  111.2 227.7 %copy-start = (f32[2,256,8,128]{1,3,2,0:T(8,128)}, f32[2,256,8,128]{1,3,2,0:T(8,128)S(1)}, u32[]{:S(2)}) copy-start(f32[2,256,8,128]{1,3,2,0:T(8,128)S(1)} %get-tuple-element.280) | copy-start | bytes 6291460
  338.9 2.2 copy-start.1
  341.2 3.1 copy-start.5
  346.5 1.0 copy-start.14
  352.1 202.9 %all-to-all-start = ((bf16[512,8,768]{0,2,1:T(8,128)(2,1)}), bf16[512,8,768]{0,2,1:T(8,128)(2,1)}, u32[]{:S(2)}, u32[]{:S(2)}) async-start(bf16[512,8,768]{0,2,1:T(8,128)(2,1)} %bitcast.155), calls=%async_computation | async-start | bytes 12582912 | tf_op jit(solution)/shard_map/all_to_all | solution.py:122
  356.9 300.8 %all-gather.13.cloned.1.call-start = ((), (), s32[]{:S(2)}) async-start(), calls=%async_computation.3 | async-start | bytes 9437184 | tf_op jit(solution)/shard_map/all_gather | solution.py:125
  563.7 3.2 copy-start.11
  566.9 3.7 copy-start.13
  566.9 3.7 copy-start.12
  576.4 8.9 %copy-start.6 = (bf16[2,256,8,128]{1,3,2,0:T(8,128)(2,1)S(1)}, bf16[2,256,8,128]{1,3,2,0:T(8,128)(2,1)}, u32[]{:S(2)}) copy-start(bf16[2,256,8,128]{1,3,2,0:T(8,128)(2,1)} %copy-done.4) | copy-start | bytes 3145732
  585.3 8.1 %copy-start.3 = (f32[2,8,256,256]{3,2,1,0:T(8,128)S(1)}, f32[2,8,256,256]{3,2,1,0:T(8,128)}, u32[]{:S(2)}) copy-start(f32[2,8,256,256]{3,2,1,0:T(8,128)} %copy-done.2) | copy-start | bytes 12582916
  607.4 8.6 %copy-start.7 = (f32[8,128,128,2]{2,3,1,0:T(2,128)S(1)}, f32[8,128,128,2]{2,3,1,0:T(2,128)}, u32[]{:S(2)}) copy-start(f32[8,128,128,2]{2,3,1,0:T(2,128)} %fusion.45) | copy-start | bytes 3145732
  616.0 4.1 copy-start.9
  616.0 4.1 copy-start.15
  (1 other events, 1.0 us)
Sparse Core Ops, SparseCore 0:
  21.8 76.1 all-gather.14
  99.6 44.6 all-gather.8
  146.5 176.2 all-gather.10
  352.3 177.9 all-gather.16
  532.3 125.4 all-gather.12
where the time goes:
time: 687 us; the launch traced here: 678 us
  waiting for transfers between devices  471 us (69%)
  matrix products  93.5 us (14%)
  local copies, waits for them, and re-layouts  46.7 us (7%)
  other arithmetic  24.7 us (4%)
  blocking collectives  22.4 us (3%)
  between operations  14.6 us (2%)
    all_to_all x1, waiting for transfers between devices, on_device(): lax.all_to_all(cotangent, 'seq', split_axis=1, concat_axis=0, tiled=True)  193 us
    all_gather x1, waiting for transfers between devices, on_device(): lax.all_gather(out_weight, 'seq', axis=1, tiled=True)  178 us
    all_gather x1, waiting for transfers between devices, on_device(): lax.all_gather(normed, 'seq', axis=0, tiled=True)  33.4 us
    all_gather x1, waiting for transfers between devices, on_device(): cotangent = lax.all_gather(grad_out, 'tp', axis=1, tiled=True)  33 us
    all_gather x2, waiting for transfers between devices, carried_in(): pieces = jax.tree.map(lambda part: lax.all_gather(part, axis), value)  32.3 us
    all_gather x1, blocking collectives, carried_in(): pieces = jax.tree.map(lambda part: lax.all_gather(part, axis), value)  22.4 us
    unnamed x46, local copies, waits for them, and re-layouts  19.6 us
    select_n x14, other arithmetic, turn(): jnp.where(position < mine, new, old)  16.8 us
  transfers between devices with their start and end apart: 6, of which 5 were waited for; matrix products, arithmetic and copies ran while one was open for 16% of the time, Pallas kernels for 0%

commit v1 on v0

v1 whole, which is shorter than its diff:
```python
import jax
import jax.numpy as jnp
from jax import lax
from jax.experimental import pallas as pl
from jax.experimental.pallas import tpu as pltpu
from jax.sharding import PartitionSpec as P

SUB = 256
EPS = 1e-06
F32 = jnp.float32
BF16 = jnp.bfloat16


def halves(x):
    high = x.astype(BF16)
    return high, (x - high.astype(F32)).astype(BF16)


def dot(a, b, ca, cb):
    return lax.dot_general(a, b, (((ca,), (cb,)), ((), ())), preferred_element_type=F32)


def wide_left(a, b, ca, cb):
    high, low = halves(a)
    return dot(high, b, ca, cb) + dot(low, b, ca, cb)


def wide_right(a, b, ca, cb):
    high, low = halves(b)
    return dot(a, high, ca, cb) + dot(a, low, ca, cb)


def wide_both(a, b, ca, cb):
    ah, al = halves(a)
    bh, bl = halves(b)
    return dot(ah, bh, ca, cb) + (dot(ah, bl, ca, cb) + dot(al, bh, ca, cb))


def decay_between(col, row, diagonal):
    weight = jnp.exp(jnp.minimum(col - row, 0.0))
    if diagonal:
        shape = weight.shape
        lower = lax.broadcasted_iota(jnp.int32, shape, 0) >= lax.broadcasted_iota(jnp.int32, shape, 1)
        weight = jnp.where(lower, weight, 0.0)
    return weight


def state_kernel(k_ref, v_ref, col_ref, state_ref):
    col = col_ref[0]
    total = col[-1:, :]
    state_ref[0] = wide_right(k_ref[...], jnp.exp(total - col) * v_ref[...].astype(F32), 0, 0)


def forward_kernel(q_ref, k_ref, v_ref, col_ref, row_ref, state_ref, att_ref, normed_ref):
    rows = q_ref.shape[0]
    state = state_ref[0]
    for t in range(0, rows, SUB):
        query = q_ref[t : t + SUB, :]
        col = col_ref[0, t : t + SUB, :]
        total = jnp.exp(col) * wide_right(query, state, 1, 0)
        for s in range(0, t + 1, SUB):
            weight = decay_between(col, row_ref[0, :, s : s + SUB], s == t)
            scores = dot(query, k_ref[s : s + SUB, :], 1, 1) * weight
            total = total + wide_left(scores, v_ref[s : s + SUB, :], 1, 0)
        att_ref[t : t + SUB, :] = total
        scale = jnp.sqrt(jnp.mean(total * total, axis=-1, keepdims=True) + EPS)
        normed_ref[t : t + SUB, :] = (total / scale).astype(BF16)


def cotangent_kernel(q_ref, col_ref, att_ref, gn_ref, ga_ref, grad_ref):
    att = att_ref[...]
    scale = jnp.sqrt(jnp.mean(att * att, axis=-1, keepdims=True) + EPS)
    o_hat = att / scale
    gn = gn_ref[...]
    ga = (gn - o_hat * jnp.mean(gn * o_hat, axis=-1, keepdims=True)) / scale
    ga_ref[...] = ga
    grad_ref[0] = wide_right(q_ref[...], jnp.exp(col_ref[0]) * ga, 0, 0)


def backward_kernel(
    q_ref, k_ref, v_ref, ga_ref, col_ref, row_ref, state_ref, end_ref, gq_ref, gk_ref, gv_ref
):
    rows = q_ref.shape[0]
    state = state_ref[0]
    end = end_ref[0]
    col_all = col_ref[0]
    into_end = jnp.exp(col_all[-1:, :] - col_all)
    starts = range(0, rows, SUB)
    gk = {}
    gv = {}
    for s in starts:
        tail = into_end[s : s + SUB, :]
        gk[s] = tail * wide_right(v_ref[s : s + SUB, :], end, 1, 1)
        gv[s] = tail * wide_right(k_ref[s : s + SUB, :], end, 1, 0)
    for t in starts:
        query = q_ref[t : t + SUB, :]
        ga = ga_ref[t : t + SUB, :]
        col = col_all[t : t + SUB, :]
        gq = jnp.exp(col) * wide_both(ga, state, 1, 1)
        for s in range(0, t + 1, SUB):
            key = k_ref[s : s + SUB, :]
            weight = decay_between(col, row_ref[0, :, s : s + SUB], s == t)
            scores = dot(query, key, 1, 1) * weight
            mix = wide_left(ga, v_ref[s : s + SUB, :], 1, 1) * weight
            gq = gq + wide_left(mix, key, 1, 0)
            gk[s] = gk[s] + wide_left(mix, query, 0, 0)
            gv[s] = gv[s] + wide_both(scores, ga, 0, 0)
        gq_ref[t : t + SUB, :] = gq.astype(BF16)
    for s in starts:
        gk_ref[s : s + SUB, :] = gk[s].astype(BF16)
        gv_ref[s : s + SUB, :] = gv[s].astype(BF16)


def per_head(kernel, heads, rows, size, ins, outs, flops):
    kinds = {
        "tok": pl.BlockSpec((rows, size), lambda h: (0, h)),
        "col": pl.BlockSpec((1, rows, 1), lambda h: (h, 0, 0)),
        "row": pl.BlockSpec((1, 1, rows), lambda h: (h, 0, 0)),
        "state": pl.BlockSpec((1, size, size), lambda h: (h, 0, 0)),
    }
    shapes = {"tok": (rows, heads * size), "state": (heads, size, size)}
    return pl.pallas_call(
        kernel,
        grid=(heads,),
        in_specs=[kinds[kind] for kind in ins],
        out_specs=[kinds[kind] for kind, _ in outs],
        out_shape=[jax.ShapeDtypeStruct(shapes[kind], dtype) for kind, dtype in outs],
        compiler_params=pltpu.CompilerParams(vmem_limit_bytes=32 * 2**20),
        cost_estimate=pl.CostEstimate(
            flops=flops, bytes_accessed=4 * rows * heads * size * 2, transcendentals=0
        ),
    )


def on_device(queries, keys, values, log_decay, out_weight, grad_out):
    rows, heads = log_decay.shape
    size = queries.shape[1] // heads
    count, mine = lax.axis_size("seq"), lax.axis_index("seq")
    tps, tp = lax.axis_size("tp"), lax.axis_index("tp")

    cumul = jnp.cumsum(log_decay.T, axis=1)
    row = cumul[:, None, :]
    col = cumul[:, :, None]
    dev_log = cumul[:, -1]
    unit = 2 * rows * heads * size * size
    (dev_state,) = per_head(
        state_kernel, heads, rows, size, ("tok", "tok", "col"), (("state", F32),), 2 * unit
    )(keys, values, col)

    below = jnp.broadcast_to(dev_log[:, None, None], (heads, 8, size))
    pieces = lax.all_gather(jnp.concatenate([dev_state, below], axis=1), "seq")
    logs = pieces[:, :, size, 0]
    place = jnp.arange(count)
    between = (place[None, :] > place[:, None]) & (place[None, :] < mine)
    early = jnp.sum(jnp.where(between[:, :, None], logs[None], 0.0), axis=1)
    early = jnp.where((place < mine)[:, None], jnp.exp(early), 0.0)
    between = (place[None, :] < place[:, None]) & (place[None, :] > mine)
    late = jnp.sum(jnp.where(between[:, :, None], logs[None], 0.0), axis=1)
    late = jnp.where((place > mine)[:, None], jnp.exp(late), 0.0)
    state_in = jnp.sum(early[:, :, None, None] * pieces[:, :, :size, :], axis=0)

    weight_all = lax.all_gather(out_weight, "seq", axis=1, tiled=True)
    cotangent = lax.all_gather(grad_out, "tp", axis=1, tiled=True)

    share = count // tps
    width = grad_out.shape[1] // share
    arrived = jnp.zeros((share, rows, width), grad_out.dtype)
    for turn in range(share):
        pairs = []
        for i in range(count):
            for j in range(tps):
                to = (share * j + (i % share + turn) % share) * tps + i // share
                pairs.append((i * tps + j, to))
        block = lax.rem(lax.rem(mine, share) + turn, share)
        piece = lax.dynamic_slice_in_dim(grad_out, block * width, width, axis=1)
        piece = lax.ppermute(piece, ("seq", "tp"), pairs)
        slot = lax.rem(lax.rem(mine, share) + share - turn, share)
        arrived = lax.dynamic_update_slice_in_dim(arrived, piece[None], slot, axis=0)
    by_columns = lax.all_gather(
        arrived.reshape(share * rows, width), "tp", axis=0, tiled=True
    )

    attended, normed = per_head(
        forward_kernel,
        heads,
        rows,
        size,
        ("tok", "tok", "tok", "col", "row", "state"),
        (("tok", F32), ("tok", BF16)),
        12 * unit,
    )(queries, keys, values, col, row, state_in)
    normed_all = lax.all_gather(normed, "seq", axis=0, tiled=True)

    grad_normed = lax.dot_general(
        cotangent, weight_all, (((1,), (1,)), ((), ())), preferred_element_type=F32
    )
    grad_att, dev_grad = per_head(
        cotangent_kernel,
        heads,
        rows,
        size,
        ("tok", "col", "tok", "tok"),
        (("tok", F32), ("state", F32)),
        2 * unit,
    )(queries, col, attended, grad_normed)
    grads = lax.all_gather(dev_grad, "seq")
    end_grad = jnp.sum(late[:, :, None, None] * grads, axis=0)
    grad_q, grad_k, grad_v = per_head(
        backward_kernel,
        heads,
        rows,
        size,
        ("tok", "tok", "tok", "tok", "col", "row", "state", "state"),
        (("tok", BF16), ("tok", BF16), ("tok", BF16)),
        40 * unit,
    )(queries, keys, values, grad_att, col, row, state_in, end_grad)
    grad_weight = lax.dot_general(
        by_columns, normed_all, (((0,), (0,)), ((), ())), preferred_element_type=F32
    )
    return grad_q, grad_k, grad_v, grad_weight


def solution(mesh):
    spec = P("seq", "tp")
    return jax.shard_map(
        on_device,
        mesh=mesh,
        in_specs=(spec, spec, spec, spec, P("tp", "seq"), spec),
        out_specs=(spec, spec, spec, spec),
        check_vma=False,
    )
```

time: 687 us -> 654 us (0.952); the launches traced: 678 us -> 653 us
  waiting for transfers between devices: 471 us -> 548 us
  matrix products: 93.5 us -> 23.7 us
  Pallas kernels: 0 us -> 35.6 us
  local copies, waits for them, and re-layouts: 46.7 us -> 17 us
  blocking collectives: 22.4 us -> 0 us
  other arithmetic: 24.7 us -> 8.92 us
    all_gather x4 -> x5, waiting for transfers between devices: 244 us -> 501 us  [the longest x1 178 us: on_device(): weight_all = lax.all_gather(out_weight, 'seq', axis=1, tiled=True)]
    all_to_all x1 -> x0, waiting for transfers between devices: 193 us -> none  [on_device(): lax.all_to_all(cotangent, 'seq', split_axis=1, concat_axis=0, tiled=True)]
    dot_general x18 -> x2, matrix products: 93.5 us -> 23.7 us  [the longest x1 12.1 us: on_device(): lax.dot_general(by_columns, normed_all, (((0,), (0,)), ((), ())), preferr...]
    pallas_call x0 -> x4, Pallas kernels: none -> 35.6 us  [the longest x1 17.6 us: on_device(): per_head(backward_kernel, heads, rows, size, ('tok', 'tok', 'tok', 'tok',...]
    all_gather x1 -> x0, blocking collectives: 22.4 us -> none  [carried_in(): pieces = jax.tree.map(lambda part: lax.all_gather(part, axis), value)]
    select_n x14 -> x2, other arithmetic: 16.8 us -> 0.14 us  [the longest x1 0.07 us: on_device(): late = jnp.where((place > mine)[:, None], jnp.exp(late), 0.0)]
    ppermute x0 -> x2, waiting for transfers between devices: none -> 14.1 us  [on_device(): piece = lax.ppermute(piece, ('seq', 'tp'), pairs)]
    unnamed x46 -> x30, local copies, waits for them, and re-layouts: 19.6 us -> 7.8 us
  transfers between devices with their start and end apart: 6 -> 8, of which waited for: 5 -> 7; matrix products, arithmetic and copies ran while one was open for 16% -> 5% of each run, Pallas kernels for 0% -> 2%
where the time goes in v1:
time: 654 us; the launch traced here: 653 us
  waiting for transfers between devices  548 us (84%)
  Pallas kernels  35.6 us (5%)
  matrix products  23.7 us (4%)
  local copies, waits for them, and re-layouts  17 us (3%)
  between operations  14.3 us (2%)
  other arithmetic  8.92 us (1%)
    all_gather x1, waiting for transfers between devices, on_device(): weight_all = lax.all_gather(out_weight, 'seq', axis=1, tiled=True)  178 us
    all_gather x1, waiting for transfers between devices, on_device(): normed_all = lax.all_gather(normed, 'seq', axis=0, tiled=True)  128 us
    all_gather x1, waiting for transfers between devices, on_device(): pieces = lax.all_gather(jnp.concatenate([dev_state, below], axis=1), 'seq')  107 us
    all_gather x1, waiting for transfers between devices, on_device(): grads = lax.all_gather(dev_grad, 'seq')  62.1 us
    all_gather x1, waiting for transfers between devices, on_device(): cotangent = lax.all_gather(grad_out, 'tp', axis=1, tiled=True)  31.6 us
    all_gather x1, waiting for transfers between devices, on_device(): lax.all_gather(arrived.reshape(share * rows, width), 'tp', axis=0, tiled=...  26.4 us
    pallas_call x1, Pallas kernels, on_device(): per_head(backward_kernel, heads, rows, size, ('tok', 'tok', 'tok', 'tok',...  17.6 us
    ppermute x2, waiting for transfers between devices, on_device(): piece = lax.ppermute(piece, ('seq', 'tp'), pairs)  14.1 us
  transfers between devices with their start and end apart: 8, of which 7 were waited for; matrix products, arithmetic and copies ran while one was open for 5% of the time, Pallas kernels for 2%

profile of v1, /device:TPU:0, one launch (start us, length us, event | category | flops | bytes accessed | tf_op | source)
XLA Modules:
  0.0 653.2 jit_solution(12636980143309692943)
XLA Ops:
  7.2 2.2 reduce-window.6
  13.1 3.5 shard_map.93
  19.1 2.6 constant_dynamic-slice_fusion
  21.7 1.8 collective-permute-start
  23.5 2.9 collective-permute-start.1
  26.4 1.2 broadcast_in_dim.89
  28.6 14.1 %collective-permute-done.1 = bf16[512,768]{1,0:T(8,128)(2,1)} collective-permute-done((bf16[512,768]{1,0:T(8,128)(2,1)}, bf16[512,768]{1,0:T(8,128)(2,1)}, u32[]{:S(2)}, u32[]{:S(2)}) %collective-permute-start.1) | collective-permute-done | bytes 786464 | tf_op jit(solution)/shard_map/ppermute | solution.py:176
  42.7 2.1 bitcast_dynamic-update-slice_fusion
  44.9 106.9 %all-gather.17.cloned.1.call-done = f32[64,136,128]{2,1,0:T(8,128)} async-done(((f32[8,136,128]{2,1,0:T(8,128)}), f32[64,136,128]{2,1,0:T(8,128)}) %all-gather.17.cloned.1.call-update) | async-done | bytes 4456464 | tf_op jit(solution)/shard_map/all_gather | solution.py:151
  151.8 1.3 slice_reduce_fusion
  153.3 2.6 fusion.state_ref
  155.9 8.8 %shard_map.94 = (f32[512,1024]{1,0:T(8,128)S(1)}, bf16[512,1024]{1,0:T(8,128)(2,1)S(1)}) custom-call(bf16[512,1024]{1,0:T(8,128)(2,1)S(1)} %copy-done.2, bf16[512,1024]{1,0:T(8,128)(2,1)S(1)} %copy-done.5, bf16[512,1024]{1,0:T(8,128)(2,1)S(1)} %copy-done.8, f32[8,512,1]{2,1,0:T(8,128)S(1)} %copy.44.col_ref, f32[8,1,512]{2,1,0:T(1,128)S(1)} %bitcast.19, ...), custom_call_target="tpu_custom_call" | custom-call | flops 1610612736 | bytes 4194304 | tf_op jit(solution)/shard_map/pallas_call | solution.py:183
  164.8 1.3 copy-done
  167.3 31.6 %all-gather.9.cloned.1.call-done = bf16[512,6144]{1,0:T(8,128)(2,1)} async-done(((bf16[512,1536]{1,0:T(8,128)(2,1)}), bf16[512,6144]{1,0:T(8,128)(2,1)}) %all-gather.9.cloned.1.call-update) | async-done | bytes 6291472 | tf_op jit(solution)/shard_map/all_gather | solution.py:163
  198.9 178.5 %all-gather.11.cloned.1.call-done = bf16[1024,6144]{1,0:T(8,128)(2,1)} async-done(((bf16[1024,768]{1,0:T(8,128)(2,1)}), bf16[1024,6144]{1,0:T(8,128)(2,1)}) %all-gather.11.cloned.1.call-update) | async-done | bytes 12582928 | tf_op jit(solution)/shard_map/all_gather | solution.py:162
  377.4 11.7 %fusion.3.gn_ref = f32[512,1024]{1,0:T(8,128)S(1)} fusion(bf16[512,6144]{1,0:T(8,128)(2,1)} %all-gather.9.cloned.1.call-done, bf16[1024,6144]{1,0:T(8,128)(2,1)} %all-gather.11.cloned.1.call-done), kind=kOutput, calls=%fused_computation.22 | convolution fusion | flops 6442450944 | bytes 20971520 | tf_op jit(solution)/shard_map/dot_general | solution.py:194
  389.1 5.7 shard_map.95
  395.5 1.4 copy-done.13
  397.0 26.4 %all-gather.13.cloned.1.call-done = bf16[4096,768]{1,0:T(8,128)(2,1)} async-done(((bf16[1024,768]{1,0:T(8,128)(2,1)}), bf16[4096,768]{1,0:T(8,128)(2,1)}) %all-gather.13.cloned.1.call-update) | async-done | bytes 6291472 | tf_op jit(solution)/shard_map/all_gather | solution.py:179
  423.4 127.5 %all-gather.15.cloned.1.call-done = bf16[4096,1024]{1,0:T(8,128)(2,1)} async-done(((bf16[512,1024]{1,0:T(8,128)(2,1)}), bf16[4096,1024]{1,0:T(8,128)(2,1)}) %all-gather.15.cloned.1.call-update) | async-done | bytes 8388624 | tf_op jit(solution)/shard_map/all_gather | solution.py:192
  550.9 12.1 %fusion.4 = f32[768,1024]{1,0:T(8,128)} fusion(bf16[4096,768]{1,0:T(8,128)(2,1)} %all-gather.13.cloned.1.call-done, bf16[4096,1024]{1,0:T(8,128)(2,1)} %all-gather.15.cloned.1.call-done), kind=kOutput, calls=%fused_computation.23 | convolution fusion | flops 6442450944 | bytes 17825792 | tf_op jit(solution)/shard_map/dot_general | solution.py:217
  563.0 62.1 %all-gather.19.cloned.1.call-done = f32[64,128,128]{2,1,0:T(8,128)} async-done(((f32[8,128,128]{2,1,0:T(8,128)}), f32[64,128,128]{2,1,0:T(8,128)}) %all-gather.19.cloned.1.call-update) | async-done | bytes 4194320 | tf_op jit(solution)/shard_map/all_gather | solution.py:206
  625.1 2.7 multiply_reduce_fusion.end_ref
  628.7 17.6 %shard_map.96 = (bf16[512,1024]{1,0:T(8,128)(2,1)}, bf16[512,1024]{1,0:T(8,128)(2,1)}, bf16[512,1024]{1,0:T(8,128)(2,1)}) custom-call(bf16[512,1024]{1,0:T(8,128)(2,1)S(1)} %copy-done.2, bf16[512,1024]{1,0:T(8,128)(2,1)S(1)} %copy-done.6, bf16[512,1024]{1,0:T(8,128)(2,1)S(1)} %copy-done.9, f32[512,1024]{1,0:T(8,128)S(1)} %copy-done.14, ...), custom_call_target="tpu_custom_call" | custom-call | flops 5368709120 | bytes 4194304 | tf_op jit(solution)/shard_map/pallas_call | solution.py:208
  (59 shorter events, 10.3 us)
Async XLA Ops:
  7.2 144.7 %all-gather.17.cloned.1.call-start = ((), (), s32[]{:S(2)}) async-start(), calls=%async_computation.4 | async-start | bytes 5013504 | tf_op jit(solution)/shard_map/all_gather | solution.py:151
  10.6 1.2 copy-start.4
  11.8 1.2 copy-start.7
  17.5 181.4 %all-gather.9.cloned.1.call-start = ((), (), s32[]{:S(2)}) async-start(), calls=%async_computation | async-start | bytes 7864320 | tf_op jit(solution)/shard_map/all_gather | solution.py:163
  18.3 359.1 %all-gather.11.cloned.1.call-start = ((), (), s32[]{:S(2)}) async-start(), calls=%async_computation.1 | async-start | bytes 14155776 | tf_op jit(solution)/shard_map/all_gather | solution.py:162
  19.0 404.4 %all-gather.13.cloned.1.call-start = ((), (), s32[]{:S(2)}) async-start(), calls=%async_computation.2 | async-start | bytes 7864320 | tf_op jit(solution)/shard_map/all_gather | solution.py:179
  21.7 4.7 collective-permute-start
  23.5 19.2 %collective-permute-start.1 = (bf16[512,768]{1,0:T(8,128)(2,1)}, bf16[512,768]{1,0:T(8,128)(2,1)}, u32[]{:S(2)}, u32[]{:S(2)}) collective-permute-start(bf16[512,768]{1,0:T(8,128)(2,1)} %get-tuple-element.20), channel_id=1, source_target_pairs={{0,4},{1,12},{2,20},{3,28},{4,0},{5,8},{6,16},{7,24},{8,5},{9,13},... | collective-permute-start | bytes 2359304 | tf_op jit(solution)/shard_map/ppermute | solution.py:176
  28.6 127.3 %copy-start.2 = (bf16[512,1024]{1,0:T(8,128)(2,1)S(1)}, bf16[512,1024]{1,0:T(8,128)(2,1)}, u32[]{:S(2)}) copy-start(bf16[512,1024]{1,0:T(8,128)(2,1)} %q_ref.5) | copy-start | bytes 3145732
  44.8 506.1 %all-gather.15.cloned.1.call-start = ((), (), s32[]{:S(2)}) async-start(), calls=%async_computation.3 | async-start | bytes 9437184 | tf_op jit(solution)/shard_map/all_gather | solution.py:192
  151.8 4.1 copy-start.5
  151.8 4.1 copy-start.8
  155.9 8.9 %copy-start.11 = (f32[8,128,128]{2,1,0:T(8,128)}, f32[8,128,128]{2,1,0:T(8,128)S(1)}, u32[]{:S(2)}) copy-start(f32[8,128,128]{2,1,0:T(8,128)S(1)} %fusion.state_ref) | copy-start | bytes 1572868
  164.8 1.3 copy-start
  166.1 1.0 copy-start.3
  167.1 458.0 %all-gather.19.cloned.1.call-start = ((), (), s32[]{:S(2)}) async-start(), calls=%async_computation.5 | async-start | bytes 4718592 | tf_op jit(solution)/shard_map/all_gather | solution.py:206
  377.4 11.7 %copy-start.1 = (f32[512,1024]{1,0:T(8,128)S(1)}, f32[512,1024]{1,0:T(8,128)}, u32[]{:S(2)}) copy-start(f32[512,1024]{1,0:T(8,128)} %copy-done) | copy-start | bytes 6291460
  394.7 0.8 copy-start.10
  395.5 1.4 copy-start.13
  625.1 2.8 copy-start.6
  625.1 2.8 copy-start.9
  625.1 2.9 copy-start.12
  625.1 3.6 copy-start.14
Sparse Core Ops, SparseCore 0:
  17.6 134.1 all-gather.16
  153.4 45.4 all-gather.8
  201.1 176.1 all-gather.10
  378.8 44.5 all-gather.12
  425.9 124.9 all-gather.14
  553.5 71.5 all-gather.18

commit v2 on v1

--- a/solution.py
+++ b/solution.py
@@ -132,11 +132,62 @@
     )
 
 
+def seq_permute(x, send):
+    count = lax.axis_size("seq")
+    pairs = [(i, send(i)) for i in range(count)]
+    return lax.ppermute(x, "seq", [(i, to) for i, to in pairs if 0 <= to < count])
+
+
+def seq_blocks(x):
+    count, mine = lax.axis_size("seq"), lax.axis_index("seq")
+    blocks = []
+    for hop in range(count // 2):
+        block = seq_permute(x, lambda i: (i + 2 * hop) % count) if hop else x
+        place = lax.rem(mine + count - 2 * hop, count)
+        blocks.append((place, block))
+        other = place + 1 - 2 * lax.rem(place, 2)
+        blocks.append((other, seq_permute(block, lambda i: i ^ 1)))
+    return blocks
+
+
+def carried_in(log, state, backward):
+    heads, size, _ = state.shape
+    count, mine = lax.axis_size("seq"), lax.axis_index("seq")
+    side = lax.rem(mine, 2)
+    near = (side == 0) if backward else (side == 1)
+
+    def packed(log, state):
+        return jnp.concatenate(
+            [state, jnp.broadcast_to(log[:, None, None], (heads, 8, size))], axis=1
+        )
+
+    def split(pack):
+        return pack[:, size, 0], pack[:, :size, :]
+
+    def decayed(log, state):
+        return jnp.exp(log)[:, None, None] * state
+
+    pair_log, pair_state = split(seq_permute(packed(log, state), lambda i: i ^ 1))
+    both = jnp.where(near, decayed(log, pair_state) + state, decayed(pair_log, state) + pair_state)
+    mine_pack = packed(log + pair_log, both)
+    total = jnp.zeros_like(state)
+    passed = jnp.zeros_like(log)
+    for hop in range(1, count // 2):
+        step = -2 * hop if backward else 2 * hop
+        far_log, far_state = split(seq_permute(mine_pack, lambda i: i + step))
+        total = total + decayed(passed, far_state)
+        passed = passed + far_log
+    return jnp.where(near, decayed(pair_log, total) + pair_state, total)
+
+
 def on_device(queries, keys, values, log_decay, out_weight, grad_out):
     rows, heads = log_decay.shape
     size = queries.shape[1] // heads
     count, mine = lax.axis_size("seq"), lax.axis_index("seq")
-    tps, tp = lax.axis_size("tp"), lax.axis_index("tp")
+    tps = lax.axis_size("tp")
+
+    cotangent = lax.all_gather(grad_out, "tp", axis=1, tiled=True)
+    weight_blocks = seq_blocks(out_weight)
 
     cumul = jnp.cumsum(log_decay.T, axis=1)
     row = cumul[:, None, :]
@@ -146,21 +197,7 @@
     (dev_state,) = per_head(
         state_kernel, heads, rows, size, ("tok", "tok", "col"), (("state", F32),), 2 * unit
     )(keys, values, col)
-
-    below = jnp.broadcast_to(dev_log[:, None, None], (heads, 8, size))
-    pieces = lax.all_gather(jnp.concatenate([dev_state, below], axis=1), "seq")
-    logs = pieces[:, :, size, 0]
-    place = jnp.arange(count)
-    between = (place[None, :] > place[:, None]) & (place[None, :] < mine)
-    early = jnp.sum(jnp.where(between[:, :, None], logs[None], 0.0), axis=1)
-    early = jnp.where((place < mine)[:, None], jnp.exp(early), 0.0)
-    between = (place[None, :] < place[:, None]) & (place[None, :] > mine)
-    late = jnp.sum(jnp.where(between[:, :, None], logs[None], 0.0), axis=1)
-    late = jnp.where((place > mine)[:, None], jnp.exp(late), 0.0)
-    state_in = jnp.sum(early[:, :, None, None] * pieces[:, :, :size, :], axis=0)
-
-    weight_all = lax.all_gather(out_weight, "seq", axis=1, tiled=True)
-    cotangent = lax.all_gather(grad_out, "tp", axis=1, tiled=True)
+    state_in = carried_in(dev_log, dev_state, False)
 
     share = count // tps
     width = grad_out.shape[1] // share
@@ -189,11 +226,14 @@
         (("tok", F32), ("tok", BF16)),
         12 * unit,
     )(queries, keys, values, col, row, state_in)
-    normed_all = lax.all_gather(normed, "seq", axis=0, tiled=True)
-
-    grad_normed = lax.dot_general(
-        cotangent, weight_all, (((1,), (1,)), ((), ())), preferred_element_type=F32
-    )
+    normed_blocks = seq_blocks(normed)
+
+    grad_normed = jnp.zeros((rows, heads * size), F32)
+    for place, block in weight_blocks:
+        part = lax.dynamic_slice_in_dim(cotangent, place * width, width, axis=1)
+        grad_normed = grad_normed + lax.dot_general(
+            part, block, (((1,), (1,)), ((), ())), preferred_element_type=F32
+        )
     grad_att, dev_grad = per_head(
         cotangent_kernel,
         heads,
@@ -203,8 +243,7 @@
         (("tok", F32), ("state", F32)),
         2 * unit,
     )(queries, col, attended, grad_normed)
-    grads = lax.all_gather(dev_grad, "seq")
-    end_grad = jnp.sum(late[:, :, None, None] * grads, axis=0)
+    end_grad = carried_in(dev_log, dev_grad, True)
     grad_q, grad_k, grad_v = per_head(
         backward_kernel,
         heads,
@@ -214,9 +253,12 @@
         (("tok", BF16), ("tok", BF16), ("tok", BF16)),
         40 * unit,
     )(queries, keys, values, grad_att, col, row, state_in, end_grad)
-    grad_weight = lax.dot_general(
-        by_columns, normed_all, (((0,), (0,)), ((), ())), preferred_element_type=F32
-    )
+    grad_weight = jnp.zeros((width, heads * size), F32)
+    for place, block in normed_blocks:
+        part = lax.dynamic_slice_in_dim(by_columns, place * rows, rows, axis=0)
+        grad_weight = grad_weight + lax.dot_general(
+            part, block, (((0,), (0,)), ((), ())), preferred_element_type=F32
+        )
     return grad_q, grad_k, grad_v, grad_weight
 
 

time: 654 us -> 572 us (0.87)
  waiting for transfers between devices: 548 us -> 218 us
  starting transfers between devices: 5.14 us -> 238 us
  matrix products: 23.7 us -> 42 us
    all_gather x4 -> x0, waiting for transfers between devices: 475 us -> none  [the longest x1 178 us: on_device(): weight_all = lax.all_gather(out_weight, 'seq', axis=1, tiled=True)]
    ppermute x0 -> x22, starting transfers between devices: none -> 227 us  [seq_permute(): lax.ppermute(x, 'seq', [(i, to) for i, to in pairs if 0 <= to < count])]
    ppermute x0 -> x22, waiting for transfers between devices: none -> 208 us  [seq_permute(): lax.ppermute(x, 'seq', [(i, to) for i, to in pairs if 0 <= to < count])]
    all_gather x1, waiting for transfers between devices: 31.6 us -> 0.01 us  [on_device(): cotangent = lax.all_gather(grad_out, 'tp', axis=1, tiled=True)]
    all_gather x1, waiting for transfers between devices: 26.4 us -> 0.02 us  [on_device(): lax.all_gather(arrived.reshape(share * rows, width), 'tp', axis=0, tiled=...]
    dot_general x2 -> x16, matrix products: 23.7 us -> 42 us  [the longest x8 21.4 us: on_device(): lax.dot_general(part, block, (((0,), (0,)), ((), ())), preferred_element_...]
  transfers between devices with their start and end apart: 8 -> 26, of which waited for: 7 -> 10; matrix products, arithmetic and copies ran while one was open for 5% -> 10% of each run, Pallas kernels for 2% -> 3%
where the time goes in v2:
time: 572 us; the launch traced here: 570 us
  starting transfers between devices  238 us (42%)
  waiting for transfers between devices  218 us (38%)
  matrix products  42 us (7%)
  Pallas kernels  36 us (6%)
  between operations  14.5 us (3%)
  other arithmetic  11.6 us (2%)
  local copies, waits for them, and re-layouts  10.9 us (2%)
    ppermute x22, starting transfers between devices, seq_permute(): lax.ppermute(x, 'seq', [(i, to) for i, to in pairs if 0 <= to < count])  227 us
    ppermute x22, waiting for transfers between devices, seq_permute(): lax.ppermute(x, 'seq', [(i, to) for i, to in pairs if 0 <= to < count])  208 us
    dot_general x8, matrix products, on_device(): lax.dot_general(part, block, (((0,), (0,)), ((), ())), preferred_element_...  21.4 us
    dot_general x8, matrix products, on_device(): lax.dot_general(part, block, (((1,), (1,)), ((), ())), preferred_element_...  20.5 us
    pallas_call x1, Pallas kernels, on_device(): per_head(backward_kernel, heads, rows, size, ('tok', 'tok', 'tok', 'tok',...  17.6 us
  transfers between devices with their start and end apart: 26, of which 10 were waited for; matrix products, arithmetic and copies ran while one was open for 10% of the time, Pallas kernels for 3%

profile of v2, /device:TPU:0, one launch (start us, length us, event | category | flops | bytes accessed | tf_op | source)
XLA Modules:
  0.0 570.3 jit_solution(15963163823769189097)
XLA Ops:
  9.8 7.4 %collective-permute-start.15 = (bf16[512,768]{1,0:T(8,128)(2,1)}, bf16[512,768]{1,0:T(8,128)(2,1)}, u32[]{:S(2)}, u32[]{:S(2)}) collective-permute-start(bf16[512,768]{1,0:T(8,128)(2,1)} %get-tuple-element.27), channel_id=1, source_target_pairs={{0,0},{1,8},{2,16},{3,24},{4,4},{5,12},{6,20},{7,28},{8,1},{9,9},{... | collective-permute-start | bytes 2359304 | tf_op jit(solution)/shard_map/ppermute | solution.py:213
  17.2 2.9 collective-permute-start.16
  21.5 8.8 %collective-permute-done.16 = bf16[512,768]{1,0:T(8,128)(2,1)S(1)} collective-permute-done((bf16[512,768]{1,0:T(8,128)(2,1)}, bf16[512,768]{1,0:T(8,128)(2,1)S(1)}, u32[]{:S(2)}, u32[]{:S(2)}) %collective-permute-start.16) | collective-permute-done | bytes 786464 | tf_op jit(solution)/shard_map/ppermute | solution.py:213
  36.1 3.5 shard_map.93
  42.3 16.1 %collective-permute-start.5 = (bf16[1024,768]{1,0:T(8,128)(2,1)}, bf16[1024,768]{1,0:T(8,128)(2,1)}, u32[]{:S(2)}, u32[]{:S(2)}) collective-permute-start(bf16[1024,768]{1,0:T(8,128)(2,1)} %param.10), channel_id=1, source_target_pairs={{0,8},{4,12},{8,16},{12,20},{16,24},{20,28},{24,0},{28,4},{1,9},{5... | collective-permute-start | bytes 4718600 | tf_op jit(solution)/shard_map/ppermute | solution.py:138
  58.4 8.9 %collective-permute-start.9 = (bf16[1024,768]{1,0:T(8,128)(2,1)}, bf16[1024,768]{1,0:T(8,128)(2,1)}, u32[]{:S(2)}, u32[]{:S(2)}) collective-permute-start(bf16[1024,768]{1,0:T(8,128)(2,1)} %param.10), channel_id=1, source_target_pairs={{0,24},{4,28},{8,0},{12,4},{16,8},{20,12},{24,16},{28,20},{1,25},{... | collective-permute-start | bytes 4718600 | tf_op jit(solution)/shard_map/ppermute | solution.py:138
  67.3 65.1 %collective-permute-start.7 = (bf16[1024,768]{1,0:T(8,128)(2,1)}, bf16[1024,768]{1,0:T(8,128)(2,1)}, u32[]{:S(2)}, u32[]{:S(2)}) collective-permute-start(bf16[1024,768]{1,0:T(8,128)(2,1)} %param.10), channel_id=1, source_target_pairs={{0,16},{4,20},{8,24},{12,28},{16,0},{20,4},{24,8},{28,12},{1,17},{... | collective-permute-start | bytes 4718600 | tf_op jit(solution)/shard_map/ppermute | solution.py:138
  135.4 13.6 %collective-permute-start.2 = (f32[8,136,128]{2,1,0:T(8,128)}, f32[8,136,128]{2,1,0:T(8,128)}, u32[]{:S(2)}, u32[]{:S(2)}) collective-permute-start(f32[8,136,128]{2,1,0:T(8,128)} %pad_maximum_fusion.2), channel_id=1, source_target_pairs={{0,16},{4,20},{8,24},{12,28},{1,17},{5,21},{9,25},{13,29},{2,18},{... | collective-permute-start | bytes 1671176 | tf_op jit(solution)/shard_map/ppermute | solution.py:138
  151.1 28.4 %collective-permute-done.2 = f32[8,136,128]{2,1,0:T(8,128)} collective-permute-done((f32[8,136,128]{2,1,0:T(8,128)}, f32[8,136,128]{2,1,0:T(8,128)}, u32[]{:S(2)}, u32[]{:S(2)}) %collective-permute-start.2) | collective-permute-done | bytes 557088 | tf_op jit(solution)/shard_map/ppermute | solution.py:138
  179.5 83.4 %collective-permute-start.3 = (f32[8,136,128]{2,1,0:T(8,128)}, f32[8,136,128]{2,1,0:T(8,128)}, u32[]{:S(2)}, u32[]{:S(2)}) collective-permute-start(f32[8,136,128]{2,1,0:T(8,128)} %pad_maximum_fusion.2), channel_id=1, source_target_pairs={{0,24},{4,28},{1,25},{5,29},{2,26},{6,30},{3,27},{7,31}} | collective-permute-start | bytes 1671176 | tf_op jit(solution)/shard_map/ppermute | solution.py:138
  266.1 5.4 collective-permute-done.3
  273.2 9.2 %shard_map.94 = (f32[512,1024]{1,0:T(8,128)S(1)}, bf16[512,1024]{1,0:T(8,128)(2,1)}) custom-call(bf16[512,1024]{1,0:T(8,128)(2,1)S(1)} %copy-done.2, bf16[512,1024]{1,0:T(8,128)(2,1)S(1)} %copy-done.6, bf16[512,1024]{1,0:T(8,128)(2,1)S(1)} %copy-done.9, f32[8,512,1]{2,1,0:T(8,128)S(1)} %copy.25.col_ref, f32[8,1,512]{2,1,0:T(1,128)S(1)} %bitcast.31, ...), custom_call_target="tpu_custom_call" | custom-call | flops 1610612736 | bytes 4194304 | tf_op jit(solution)/shard_map/pallas_call | solution.py:220
  283.7 4.3 collective-permute-start.22
  300.5 33.9 %collective-permute-done.6 = bf16[1024,768]{1,0:T(8,128)(2,1)} collective-permute-done((bf16[1024,768]{1,0:T(8,128)(2,1)}, bf16[1024,768]{1,0:T(8,128)(2,1)}, u32[]{:S(2)}, u32[]{:S(2)}) %collective-permute-start.6) | collective-permute-done | bytes 1572896 | tf_op jit(solution)/shard_map/ppermute | solution.py:138
  334.4 18.5 %collective-permute-start.20 = (bf16[512,1024]{1,0:T(8,128)(2,1)}, bf16[512,1024]{1,0:T(8,128)(2,1)}, u32[]{:S(2)}, u32[]{:S(2)}) collective-permute-start(bf16[512,1024]{1,0:T(8,128)(2,1)} %get-tuple-element.17), channel_id=1, source_target_pairs={{0,16},{4,20},{8,24},{12,28},{16,0},{20,4},{24,8},{28,12},{1,17},{... | collective-permute-start | bytes 3145736 | tf_op jit(solution)/shard_map/ppermute | solution.py:138
  358.1 39.4 %collective-permute-done.8 = bf16[1024,768]{1,0:T(8,128)(2,1)} collective-permute-done((bf16[1024,768]{1,0:T(8,128)(2,1)}, bf16[1024,768]{1,0:T(8,128)(2,1)}, u32[]{:S(2)}, u32[]{:S(2)}) %collective-permute-start.8) | collective-permute-done | bytes 1572896 | tf_op jit(solution)/shard_map/ppermute | solution.py:138
  402.9 5.7 shard_map.95
  413.4 3.3 collective-permute-done.20
  418.7 7.9 %collective-permute-done.11 = f32[8,136,128]{2,1,0:T(8,128)S(1)} collective-permute-done((f32[8,136,128]{2,1,0:T(8,128)}, f32[8,136,128]{2,1,0:T(8,128)S(1)}, u32[]{:S(2)}, u32[]{:S(2)}) %collective-permute-start.11) | collective-permute-done | bytes 557088 | tf_op jit(solution)/shard_map/ppermute | solution.py:138
  438.8 10.4 %collective-permute-done.17 = bf16[512,1024]{1,0:T(8,128)(2,1)} collective-permute-done((bf16[512,1024]{1,0:T(8,128)(2,1)}, bf16[512,1024]{1,0:T(8,128)(2,1)}, u32[]{:S(2)}, u32[]{:S(2)}) %collective-permute-start.17) | collective-permute-done | bytes 1048608 | tf_op jit(solution)/shard_map/ppermute | solution.py:138
  452.7 58.6 %collective-permute-done.19 = bf16[512,1024]{1,0:T(8,128)(2,1)} collective-permute-done((bf16[512,1024]{1,0:T(8,128)(2,1)}, bf16[512,1024]{1,0:T(8,128)(2,1)}, u32[]{:S(2)}, u32[]{:S(2)}) %collective-permute-start.19) | collective-permute-done | bytes 1048608 | tf_op jit(solution)/shard_map/ppermute | solution.py:138
  517.4 5.1 add_add_fusion
  522.5 20.8 %collective-permute-done.12 = f32[8,136,128]{2,1,0:T(8,128)} collective-permute-done((f32[8,136,128]{2,1,0:T(8,128)}, f32[8,136,128]{2,1,0:T(8,128)}, u32[]{:S(2)}, u32[]{:S(2)}) %collective-permute-start.12) | collective-permute-done | bytes 557088 | tf_op jit(solution)/shard_map/ppermute | solution.py:138
  545.9 17.6 %shard_map.96 = (bf16[512,1024]{1,0:T(8,128)(2,1)}, bf16[512,1024]{1,0:T(8,128)(2,1)}, bf16[512,1024]{1,0:T(8,128)(2,1)}) custom-call(bf16[512,1024]{1,0:T(8,128)(2,1)S(1)} %copy-done.4, bf16[512,1024]{1,0:T(8,128)(2,1)S(1)} %copy-done.7, bf16[512,1024]{1,0:T(8,128)(2,1)S(1)} %copy-done.10, f32[512,1024]{1,0:T(8,128)S(1)} %copy-done.14, ...), custom_call_target="tpu_custom_call" | custom-call | flops 5368709120 | bytes 4194304 | tf_op jit(solution)/shard_map/pallas_call | solution.py:247
  (120 shorter events, 77.6 us)
Async XLA Ops:
  7.2 282.9 %all-gather.3.cloned.1.call-start = ((), (), s32[]{:S(2)}) async-start(), calls=%async_computation | async-start | bytes 7864320 | tf_op jit(solution)/shard_map/all_gather | solution.py:189
  7.9 421.2 %all-gather.5.cloned.1.call-start = ((), (), s32[]{:S(2)}) async-start(), calls=%async_computation.1 | async-start | bytes 7864320 | tf_op jit(solution)/shard_map/all_gather | solution.py:216
  40.0 92.3 %collective-permute-start = (f32[8,136,128]{2,1,0:T(8,128)S(1)}, f32[8,136,128]{2,1,0:T(8,128)}, u32[]{:S(2)}, u32[]{:S(2)}) collective-permute-start(f32[8,136,128]{2,1,0:T(8,128)S(1)} %pad_maximum_fusion.1), channel_id=1, source_target_pairs={{0,4},{4,0},{8,12},{12,8},{16,20},{20,16},{24,28},{28,24},{1,5},{5... | collective-permute-start | bytes 1671176 | tf_op jit(solution)/shard_map/ppermute | solution.py:138
  42.3 222.2 %collective-permute-start.5 = (bf16[1024,768]{1,0:T(8,128)(2,1)}, bf16[1024,768]{1,0:T(8,128)(2,1)}, u32[]{:S(2)}, u32[]{:S(2)}) collective-permute-start(bf16[1024,768]{1,0:T(8,128)(2,1)} %param.10), channel_id=1, source_target_pairs={{0,8},{4,12},{8,16},{12,20},{16,24},{20,28},{24,0},{28,4},{1,9},{5... | collective-permute-start | bytes 4718600 | tf_op jit(solution)/shard_map/ppermute | solution.py:138
  58.4 229.7 %collective-permute-start.9 = (bf16[1024,768]{1,0:T(8,128)(2,1)}, bf16[1024,768]{1,0:T(8,128)(2,1)}, u32[]{:S(2)}, u32[]{:S(2)}) collective-permute-start(bf16[1024,768]{1,0:T(8,128)(2,1)} %param.10), channel_id=1, source_target_pairs={{0,24},{4,28},{8,0},{12,4},{16,8},{20,12},{24,16},{28,20},{1,25},{... | collective-permute-start | bytes 4718600 | tf_op jit(solution)/shard_map/ppermute | solution.py:138
  67.3 221.3 %collective-permute-start.7 = (bf16[1024,768]{1,0:T(8,128)(2,1)}, bf16[1024,768]{1,0:T(8,128)(2,1)}, u32[]{:S(2)}, u32[]{:S(2)}) collective-permute-start(bf16[1024,768]{1,0:T(8,128)(2,1)} %param.10), channel_id=1, source_target_pairs={{0,16},{4,20},{8,24},{12,28},{16,0},{20,4},{24,8},{28,12},{1,17},{... | collective-permute-start | bytes 4718600 | tf_op jit(solution)/shard_map/ppermute | solution.py:138
  135.4 44.0 %collective-permute-start.2 = (f32[8,136,128]{2,1,0:T(8,128)}, f32[8,136,128]{2,1,0:T(8,128)}, u32[]{:S(2)}, u32[]{:S(2)}) collective-permute-start(f32[8,136,128]{2,1,0:T(8,128)} %pad_maximum_fusion.2), channel_id=1, source_target_pairs={{0,16},{4,20},{8,24},{12,28},{1,17},{5,21},{9,25},{13,29},{2,18},{... | collective-permute-start | bytes 1671176 | tf_op jit(solution)/shard_map/ppermute | solution.py:138
  149.0 114.0 %collective-permute-start.1 = (f32[8,136,128]{2,1,0:T(8,128)}, f32[8,136,128]{2,1,0:T(8,128)}, u32[]{:S(2)}, u32[]{:S(2)}) collective-permute-start(f32[8,136,128]{2,1,0:T(8,128)} %pad_maximum_fusion.2), channel_id=1, source_target_pairs={{0,8},{4,12},{8,16},{12,20},{16,24},{20,28},{1,9},{5,13},{9,17},{1... | collective-permute-start | bytes 1671176 | tf_op jit(solution)/shard_map/ppermute | solution.py:138
  179.5 92.0 %collective-permute-start.3 = (f32[8,136,128]{2,1,0:T(8,128)}, f32[8,136,128]{2,1,0:T(8,128)}, u32[]{:S(2)}, u32[]{:S(2)}) collective-permute-start(f32[8,136,128]{2,1,0:T(8,128)} %pad_maximum_fusion.2), channel_id=1, source_target_pairs={{0,24},{4,28},{1,25},{5,29},{2,26},{6,30},{3,27},{7,31}} | collective-permute-start | bytes 1671176 | tf_op jit(solution)/shard_map/ppermute | solution.py:138
  263.0 92.4 %collective-permute-start.4 = (bf16[1024,768]{1,0:T(8,128)(2,1)}, bf16[1024,768]{1,0:T(8,128)(2,1)}, u32[]{:S(2)}, u32[]{:S(2)}) collective-permute-start(bf16[1024,768]{1,0:T(8,128)(2,1)} %param.10), channel_id=1, source_target_pairs={{0,4},{4,0},{8,12},{12,8},{16,20},{20,16},{24,28},{28,24},{1,5},{5... | collective-permute-start | bytes 4718600 | tf_op jit(solution)/shard_map/ppermute | solution.py:138
  264.6 69.9 %collective-permute-start.6 = (bf16[1024,768]{1,0:T(8,128)(2,1)}, bf16[1024,768]{1,0:T(8,128)(2,1)}, u32[]{:S(2)}, u32[]{:S(2)}) collective-permute-start(bf16[1024,768]{1,0:T(8,128)(2,1)} %collective-permute-done.5), channel_id=1, source_target_pairs={{0,4},{4,0},{8,12},{12,8},{16,20},{20,16},{24,28},{28,24},{1,5},{5... | collective-permute-start | bytes 4718600 | tf_op jit(solution)/shard_map/ppermute | solution.py:138
  283.7 129.1 %collective-permute-start.22 = (bf16[512,1024]{1,0:T(8,128)(2,1)}, bf16[512,1024]{1,0:T(8,128)(2,1)}, u32[]{:S(2)}, u32[]{:S(2)}) collective-permute-start(bf16[512,1024]{1,0:T(8,128)(2,1)} %get-tuple-element.17), channel_id=1, source_target_pairs={{0,24},{4,28},{8,0},{12,4},{16,8},{20,12},{24,16},{28,20},{1,25},{... | collective-permute-start | bytes 3145736 | tf_op jit(solution)/shard_map/ppermute | solution.py:138
  288.1 111.9 %collective-permute-start.10 = (bf16[1024,768]{1,0:T(8,128)(2,1)}, bf16[1024,768]{1,0:T(8,128)(2,1)}, u32[]{:S(2)}, u32[]{:S(2)}) collective-permute-start(bf16[1024,768]{1,0:T(8,128)(2,1)} %collective-permute-done.9), channel_id=1, source_target_pairs={{0,4},{4,0},{8,12},{12,8},{16,20},{20,16},{24,28},{28,24},{1,5},{5... | collective-permute-start | bytes 4718600 | tf_op jit(solution)/shard_map/ppermute | solution.py:138
  288.6 108.9 %collective-permute-start.8 = (bf16[1024,768]{1,0:T(8,128)(2,1)}, bf16[1024,768]{1,0:T(8,128)(2,1)}, u32[]{:S(2)}, u32[]{:S(2)}) collective-permute-start(bf16[1024,768]{1,0:T(8,128)(2,1)} %collective-permute-done.7), channel_id=1, source_target_pairs={{0,4},{4,0},{8,12},{12,8},{16,20},{20,16},{24,28},{28,24},{1,5},{5... | collective-permute-start | bytes 4718600 | tf_op jit(solution)/shard_map/ppermute | solution.py:138
  334.4 82.2 %collective-permute-start.20 = (bf16[512,1024]{1,0:T(8,128)(2,1)}, bf16[512,1024]{1,0:T(8,128)(2,1)}, u32[]{:S(2)}, u32[]{:S(2)}) collective-permute-start(bf16[512,1024]{1,0:T(8,128)(2,1)} %get-tuple-element.17), channel_id=1, source_target_pairs={{0,16},{4,20},{8,24},{12,28},{16,0},{20,4},{24,8},{28,12},{1,17},{... | collective-permute-start | bytes 3145736 | tf_op jit(solution)/shard_map/ppermute | solution.py:138
  355.4 61.8 %collective-permute-start.18 = (bf16[512,1024]{1,0:T(8,128)(2,1)}, bf16[512,1024]{1,0:T(8,128)(2,1)}, u32[]{:S(2)}, u32[]{:S(2)}) collective-permute-start(bf16[512,1024]{1,0:T(8,128)(2,1)} %get-tuple-element.17), channel_id=1, source_target_pairs={{0,8},{4,12},{8,16},{12,20},{16,24},{20,28},{24,0},{28,4},{1,9},{5... | collective-permute-start | bytes 3145736 | tf_op jit(solution)/shard_map/ppermute | solution.py:138
  410.8 15.8 %collective-permute-start.11 = (f32[8,136,128]{2,1,0:T(8,128)}, f32[8,136,128]{2,1,0:T(8,128)S(1)}, u32[]{:S(2)}, u32[]{:S(2)}) collective-permute-start(f32[8,136,128]{2,1,0:T(8,128)} %pad_maximum_fusion), channel_id=1, source_target_pairs={{0,4},{4,0},{8,12},{12,8},{16,20},{20,16},{24,28},{28,24},{1,5},{5... | collective-permute-start | bytes 1671176 | tf_op jit(solution)/shard_map/ppermute | solution.py:138
  411.4 37.8 %collective-permute-start.17 = (bf16[512,1024]{1,0:T(8,128)(2,1)}, bf16[512,1024]{1,0:T(8,128)(2,1)}, u32[]{:S(2)}, u32[]{:S(2)}) collective-permute-start(bf16[512,1024]{1,0:T(8,128)(2,1)} %get-tuple-element.17), channel_id=1, source_target_pairs={{0,4},{4,0},{8,12},{12,8},{16,20},{20,16},{24,28},{28,24},{1,5},{5... | collective-permute-start | bytes 3145736 | tf_op jit(solution)/shard_map/ppermute | solution.py:138
  412.8 104.5 %collective-permute-start.23 = (bf16[512,1024]{1,0:T(8,128)(2,1)}, bf16[512,1024]{1,0:T(8,128)(2,1)}, u32[]{:S(2)}, u32[]{:S(2)}) collective-permute-start(bf16[512,1024]{1,0:T(8,128)(2,1)} %collective-permute-done.22), channel_id=1, source_target_pairs={{0,4},{4,0},{8,12},{12,8},{16,20},{20,16},{24,28},{28,24},{1,5},{5... | collective-permute-start | bytes 3145736 | tf_op jit(solution)/shard_map/ppermute | solution.py:138
  416.7 98.4 %collective-permute-start.21 = (bf16[512,1024]{1,0:T(8,128)(2,1)}, bf16[512,1024]{1,0:T(8,128)(2,1)}, u32[]{:S(2)}, u32[]{:S(2)}) collective-permute-start(bf16[512,1024]{1,0:T(8,128)(2,1)} %collective-permute-done.20), channel_id=1, source_target_pairs={{0,4},{4,0},{8,12},{12,8},{16,20},{20,16},{24,28},{28,24},{1,5},{5... | collective-permute-start | bytes 3145736 | tf_op jit(solution)/shard_map/ppermute | solution.py:138
  417.2 94.1 %collective-permute-start.19 = (bf16[512,1024]{1,0:T(8,128)(2,1)}, bf16[512,1024]{1,0:T(8,128)(2,1)}, u32[]{:S(2)}, u32[]{:S(2)}) collective-permute-start(bf16[512,1024]{1,0:T(8,128)(2,1)} %collective-permute-done.18), channel_id=1, source_target_pairs={{0,4},{4,0},{8,12},{12,8},{16,20},{20,16},{24,28},{28,24},{1,5},{5... | collective-permute-start | bytes 3145736 | tf_op jit(solution)/shard_map/ppermute | solution.py:138
  427.8 116.4 %collective-permute-start.14 = (f32[8,136,128]{2,1,0:T(8,128)}, f32[8,136,128]{2,1,0:T(8,128)}, u32[]{:S(2)}, u32[]{:S(2)}) collective-permute-start(f32[8,136,128]{2,1,0:T(8,128)} %pad_maximum_fusion.3), channel_id=1, source_target_pairs={{24,0},{28,4},{25,1},{29,5},{26,2},{30,6},{27,3},{31,7}} | collective-permute-start | bytes 1671176 | tf_op jit(solution)/shard_map/ppermute | solution.py:138
  449.2 73.3 %collective-permute-start.13 = (f32[8,136,128]{2,1,0:T(8,128)}, f32[8,136,128]{2,1,0:T(8,128)}, u32[]{:S(2)}, u32[]{:S(2)}) collective-permute-start(f32[8,136,128]{2,1,0:T(8,128)} %pad_maximum_fusion.3), channel_id=1, source_target_pairs={{16,0},{20,4},{24,8},{28,12},{17,1},{21,5},{25,9},{29,13},{18,2},{... | collective-permute-start | bytes 1671176 | tf_op jit(solution)/shard_map/ppermute | solution.py:138
  511.3 32.0 %collective-permute-start.12 = (f32[8,136,128]{2,1,0:T(8,128)}, f32[8,136,128]{2,1,0:T(8,128)}, u32[]{:S(2)}, u32[]{:S(2)}) collective-permute-start(f32[8,136,128]{2,1,0:T(8,128)} %pad_maximum_fusion.3), channel_id=1, source_target_pairs={{8,0},{12,4},{16,8},{20,12},{24,16},{28,20},{9,1},{13,5},{17,9},{2... | collective-permute-start | bytes 1671176 | tf_op jit(solution)/shard_map/ppermute | solution.py:138
  (22 other events, 354.7 us)
Sparse Core Ops, SparseCore 0:
  9.6 69.1 all-gather.2
  80.3 85.0 all-gather.4

commit v3 on v2

--- a/solution.py
+++ b/solution.py
@@ -138,15 +138,17 @@
     return lax.ppermute(x, "seq", [(i, to) for i, to in pairs if 0 <= to < count])
 
 
-def seq_blocks(x):
-    count, mine = lax.axis_size("seq"), lax.axis_index("seq")
+def tp_blocks(x):
+    count, mine = lax.axis_size("tp"), lax.axis_index("tp")
     blocks = []
     for hop in range(count // 2):
-        block = seq_permute(x, lambda i: (i + 2 * hop) % count) if hop else x
+        block = x
+        if hop:
+            block = lax.ppermute(x, "tp", [(i, (i + 2 * hop) % count) for i in range(count)])
         place = lax.rem(mine + count - 2 * hop, count)
         blocks.append((place, block))
         other = place + 1 - 2 * lax.rem(place, 2)
-        blocks.append((other, seq_permute(block, lambda i: i ^ 1)))
+        blocks.append((other, lax.ppermute(block, "tp", [(i, i ^ 1) for i in range(count)])))
     return blocks
 
 
@@ -186,8 +188,8 @@
     count, mine = lax.axis_size("seq"), lax.axis_index("seq")
     tps = lax.axis_size("tp")
 
-    cotangent = lax.all_gather(grad_out, "tp", axis=1, tiled=True)
-    weight_blocks = seq_blocks(out_weight)
+    weight_all = lax.all_gather(out_weight, "seq", axis=1, tiled=True)
+    cotangent = tp_blocks(grad_out)
 
     cumul = jnp.cumsum(log_decay.T, axis=1)
     row = cumul[:, None, :]
@@ -199,6 +201,7 @@
     )(keys, values, col)
     state_in = carried_in(dev_log, dev_state, False)
 
+    grad_out, state_in = lax.optimization_barrier((grad_out, state_in))
     share = count // tps
     width = grad_out.shape[1] // share
     arrived = jnp.zeros((share, rows, width), grad_out.dtype)
@@ -213,9 +216,7 @@
         piece = lax.ppermute(piece, ("seq", "tp"), pairs)
         slot = lax.rem(lax.rem(mine, share) + share - turn, share)
         arrived = lax.dynamic_update_slice_in_dim(arrived, piece[None], slot, axis=0)
-    by_columns = lax.all_gather(
-        arrived.reshape(share * rows, width), "tp", axis=0, tiled=True
-    )
+    by_columns = tp_blocks(arrived.reshape(share * rows, width))
 
     attended, normed = per_head(
         forward_kernel,
@@ -226,13 +227,24 @@
         (("tok", F32), ("tok", BF16)),
         12 * unit,
     )(queries, keys, values, col, row, state_in)
-    normed_blocks = seq_blocks(normed)
+    own_cot, own_columns = [cotangent[0][1]], [by_columns[0][1]]
+    normed, weight_all, late_cot, late_columns = lax.optimization_barrier(
+        (
+            normed,
+            weight_all,
+            [block for _, block in cotangent[1:]],
+            [block for _, block in by_columns[1:]],
+        )
+    )
+    cotangent = [(at, x) for (at, _), x in zip(cotangent, own_cot + late_cot)]
+    by_columns = [(at, x) for (at, _), x in zip(by_columns, own_columns + late_columns)]
+    normed_all = lax.all_gather(normed, "seq", axis=0, tiled=True)
 
     grad_normed = jnp.zeros((rows, heads * size), F32)
-    for place, block in weight_blocks:
-        part = lax.dynamic_slice_in_dim(cotangent, place * width, width, axis=1)
+    for place, block in cotangent:
+        part = lax.dynamic_slice_in_dim(weight_all, place * share * width, share * width, axis=1)
         grad_normed = grad_normed + lax.dot_general(
-            part, block, (((1,), (1,)), ((), ())), preferred_element_type=F32
+            block, part, (((1,), (1,)), ((), ())), preferred_element_type=F32
         )
     grad_att, dev_grad = per_head(
         cotangent_kernel,
@@ -254,10 +266,10 @@
         40 * unit,
     )(queries, keys, values, grad_att, col, row, state_in, end_grad)
     grad_weight = jnp.zeros((width, heads * size), F32)
-    for place, block in normed_blocks:
-        part = lax.dynamic_slice_in_dim(by_columns, place * rows, rows, axis=0)
+    for place, block in by_columns:
+        part = lax.dynamic_slice_in_dim(normed_all, place * share * rows, share * rows, axis=0)
         grad_weight = grad_weight + lax.dot_general(
-            part, block, (((0,), (0,)), ((), ())), preferred_element_type=F32
+            block, part, (((0,), (0,)), ((), ())), preferred_element_type=F32
         )
     return grad_q, grad_k, grad_v, grad_weight
 

time: 572 us -> 512 us (0.90)
  starting transfers between devices: 238 us -> 185 us
  matrix products: 42 us -> 25.8 us
  local copies, waits for them, and re-layouts: 10.9 us -> 16.7 us
    ppermute x22 -> x8, starting transfers between devices: 227 us -> 19.5 us  [seq_permute(): lax.ppermute(x, 'seq', [(i, to) for i, to in pairs if 0 <= to < count])]
    ppermute x0 -> x6, starting transfers between devices: none -> 157 us  [the longest x2 156 us: tp_blocks(): lax.ppermute(x, 'tp', [(i, (i + 2 * hop) % count) for i in range(count)])]
    ppermute x22 -> x8, waiting for transfers between devices: 208 us -> 163 us  [seq_permute(): lax.ppermute(x, 'seq', [(i, to) for i, to in pairs if 0 <= to < count])]
    all_gather x2, waiting for transfers between devices: 0.02 us -> 38.1 us  [the longest x1 38.1 us: on_device(): normed_all = lax.all_gather(normed, 'seq', axis=0, tiled=True)]
    ppermute x0 -> x6, waiting for transfers between devices: none -> 17.9 us  [the longest x2 17.9 us: tp_blocks(): lax.ppermute(x, 'tp', [(i, (i + 2 * hop) % count) for i in range(count)])]
    dot_general x16 -> x8, matrix products: 42 us -> 25.8 us  [the longest x4 13 us: on_device(): lax.dot_general(block, part, (((1,), (1,)), ((), ())), preferred_element_...]
    ppermute x2, waiting for transfers between devices: 8.79 us -> 1.18 us  [on_device(): piece = lax.ppermute(piece, ('seq', 'tp'), pairs)]
  transfers between devices with their start and end apart: 26 -> 18, of which waited for: 10 -> 10; matrix products, arithmetic and copies ran while one was open for 10% -> 6% of each run, Pallas kernels for 3% -> 7%
where the time goes in v3:
time: 512 us; the launch traced here: 511 us
  waiting for transfers between devices  221 us (43%)
  starting transfers between devices  185 us (36%)
  Pallas kernels  36 us (7%)
  matrix products  25.8 us (5%)
  local copies, waits for them, and re-layouts  16.7 us (3%)
  between operations  14.5 us (3%)
  other arithmetic  11.8 us (2%)
    ppermute x8, waiting for transfers between devices, seq_permute(): lax.ppermute(x, 'seq', [(i, to) for i, to in pairs if 0 <= to < count])  163 us
    ppermute x2, starting transfers between devices, tp_blocks(): lax.ppermute(x, 'tp', [(i, (i + 2 * hop) % count) for i in range(count)])  156 us
    all_gather x1, waiting for transfers between devices, on_device(): normed_all = lax.all_gather(normed, 'seq', axis=0, tiled=True)  38.1 us
    ppermute x8, starting transfers between devices, seq_permute(): lax.ppermute(x, 'seq', [(i, to) for i, to in pairs if 0 <= to < count])  19.5 us
    ppermute x2, waiting for transfers between devices, tp_blocks(): lax.ppermute(x, 'tp', [(i, (i + 2 * hop) % count) for i in range(count)])  17.9 us
    pallas_call x1, Pallas kernels, on_device(): per_head(backward_kernel, heads, rows, size, ('tok', 'tok', 'tok', 'tok',...  17.6 us
    dot_general x4, matrix products, on_device(): lax.dot_general(block, part, (((1,), (1,)), ((), ())), preferred_element_...  13 us
    dot_general x4, matrix products, on_device(): lax.dot_general(block, part, (((0,), (0,)), ((), ())), preferred_element_...  12.8 us
  transfers between devices with their start and end apart: 18, of which 10 were waited for; matrix products, arithmetic and copies ran while one was open for 6% of the time, Pallas kernels for 7%

profile of v3, /device:TPU:0, one launch (start us, length us, event | category | flops | bytes accessed | tf_op | source)
XLA Modules:
  0.0 510.7 jit_solution(7008094783415588524)
XLA Ops:
  13.5 3.5 shard_map.93
  18.2 2.9 collective-permute-start
  21.2 24.1 %collective-permute-done = f32[8,136,128]{2,1,0:T(8,128)S(1)} collective-permute-done((f32[8,136,128]{2,1,0:T(8,128)}, f32[8,136,128]{2,1,0:T(8,128)S(1)}, u32[]{:S(2)}, u32[]{:S(2)}) %collective-permute-start) | collective-permute-done | bytes 557088 | tf_op jit(solution)/shard_map/ppermute | solution.py:138
  45.7 5.3 %collective-permute-start.2 = (f32[8,136,128]{2,1,0:T(8,128)S(1)}, f32[8,136,128]{2,1,0:T(8,128)}, u32[]{:S(2)}, u32[]{:S(2)}) collective-permute-start(f32[8,136,128]{2,1,0:T(8,128)S(1)} %pad_maximum_fusion.2), channel_id=1, source_target_pairs={{0,16},{4,20},{8,24},{12,28},{1,17},{5,21},{9,25},{13,29},{2,18},{... | collective-permute-start | bytes 1671176 | tf_op jit(solution)/shard_map/ppermute | solution.py:138
  51.0 4.4 collective-permute-start.1
  57.5 17.6 %collective-permute-done.2 = f32[8,136,128]{2,1,0:T(8,128)} collective-permute-done((f32[8,136,128]{2,1,0:T(8,128)S(1)}, f32[8,136,128]{2,1,0:T(8,128)}, u32[]{:S(2)}, u32[]{:S(2)}) %collective-permute-start.2) | collective-permute-done | bytes 557088 | tf_op jit(solution)/shard_map/ppermute | solution.py:138
  75.1 23.9 %collective-permute-done.1 = f32[8,136,128]{2,1,0:T(8,128)} collective-permute-done((f32[8,136,128]{2,1,0:T(8,128)S(1)}, f32[8,136,128]{2,1,0:T(8,128)}, u32[]{:S(2)}, u32[]{:S(2)}) %collective-permute-start.1) | collective-permute-done | bytes 557088 | tf_op jit(solution)/shard_map/ppermute | solution.py:138
  99.9 10.2 %collective-permute-done.3 = f32[8,136,128]{2,1,0:T(8,128)} collective-permute-done((f32[8,136,128]{2,1,0:T(8,128)S(1)}, f32[8,136,128]{2,1,0:T(8,128)}, u32[]{:S(2)}, u32[]{:S(2)}) %collective-permute-start.3) | collective-permute-done | bytes 557088 | tf_op jit(solution)/shard_map/ppermute | solution.py:138
  111.7 2.8 constant_dynamic-slice_fusion
  114.5 7.5 %collective-permute-start.7 = (bf16[512,768]{1,0:T(8,128)(2,1)}, bf16[512,768]{1,0:T(8,128)(2,1)}, u32[]{:S(2)}, u32[]{:S(2)}) collective-permute-start(bf16[512,768]{1,0:T(8,128)(2,1)} %get-tuple-element.47), channel_id=1, source_target_pairs={{0,0},{1,8},{2,16},{3,24},{4,4},{5,12},{6,20},{7,28},{8,1},{9,9},{... | collective-permute-start | bytes 2359304 | tf_op jit(solution)/shard_map/ppermute | solution.py:216
  123.3 26.0 %collective-permute-start.5 = (bf16[512,1536]{1,0:T(8,128)(2,1)}, bf16[512,1536]{1,0:T(8,128)(2,1)}, u32[]{:S(2)}, u32[]{:S(2)}) collective-permute-start(bf16[512,1536]{1,0:T(8,128)(2,1)} %param.11), channel_id=1, source_target_pairs={{0,2},{1,3},{2,0},{3,1},{4,6},{5,7},{6,4},{7,5},{8,10},{9,11},{10,... | collective-permute-start | bytes 4718600 | tf_op jit(solution)/shard_map/ppermute | solution.py:147
  153.2 130.3 %collective-permute-start.10 = (bf16[1024,768]{1,0:T(8,128)(2,1)S(1)}, bf16[1024,768]{1,0:T(8,128)(2,1)S(1)}, u32[]{:S(2)}, u32[]{:S(2)}) collective-permute-start(bf16[1024,768]{1,0:T(8,128)(2,1)S(1)} %bitcast.31), channel_id=1, source_target_pairs={{0,2},{1,3},{2,0},{3,1},{4,6},{5,7},{6,4},{7,5},{8,10},{9,11},{10,... | collective-permute-start | bytes 4718600 | tf_op jit(solution)/shard_map/ppermute | solution.py:147
  284.0 17.9 %collective-permute-done.10 = bf16[1024,768]{1,0:T(8,128)(2,1)S(1)} collective-permute-done((bf16[1024,768]{1,0:T(8,128)(2,1)S(1)}, bf16[1024,768]{1,0:T(8,128)(2,1)S(1)}, u32[]{:S(2)}, u32[]{:S(2)}) %collective-permute-start.10) | collective-permute-done | bytes 1572896 | tf_op jit(solution)/shard_map/ppermute | solution.py:147
  302.0 9.2 %shard_map.94 = (f32[512,1024]{1,0:T(8,128)S(1)}, bf16[512,1024]{1,0:T(8,128)(2,1)}) custom-call(bf16[512,1024]{1,0:T(8,128)(2,1)S(1)} %copy-done.2, bf16[512,1024]{1,0:T(8,128)(2,1)S(1)} %copy-done.6, bf16[512,1024]{1,0:T(8,128)(2,1)S(1)} %copy-done.9, f32[8,512,1]{2,1,0:T(8,128)S(1)} %copy.28.col_ref, f32[8,1,512]{2,1,0:T(1,128)S(1)} %bitcast.29, ...), custom_call_target="tpu_custom_call" | custom-call | flops 1610612736 | bytes 4194304 | tf_op jit(solution)/shard_map/pallas_call | solution.py:221
  315.5 4.3 fusion.6
  319.8 4.8 fusion.2
  328.6 5.7 %shard_map.95 = (f32[512,1024]{1,0:T(8,128)S(1)}, f32[8,128,128]{2,1,0:T(8,128)S(1)}) custom-call(bf16[512,1024]{1,0:T(8,128)(2,1)S(1)} %copy-done.3, f32[8,512,1]{2,1,0:T(8,128)S(1)} %copy.28.col_ref, f32[512,1024]{1,0:T(8,128)S(1)} %copy-done.1, f32[512,1024]{1,0:T(8,128)S(1)} %fusion.9.gn_ref), custom_call_target="tpu_custom_call" | custom-call | flops 268435456 | bytes 4194304 | tf_op jit(solution)/shard_map/pallas_call | solution.py:249
  336.4 25.7 %collective-permute-done.12 = f32[8,136,128]{2,1,0:T(8,128)} collective-permute-done((f32[8,136,128]{2,1,0:T(8,128)S(1)}, f32[8,136,128]{2,1,0:T(8,128)}, u32[]{:S(2)}, u32[]{:S(2)}) %collective-permute-start.12) | collective-permute-done | bytes 557088 | tf_op jit(solution)/shard_map/ppermute | solution.py:138
  369.3 36.0 %collective-permute-done.14 = f32[8,136,128]{2,1,0:T(8,128)} collective-permute-done((f32[8,136,128]{2,1,0:T(8,128)}, f32[8,136,128]{2,1,0:T(8,128)}, u32[]{:S(2)}, u32[]{:S(2)}) %collective-permute-start.14) | collective-permute-done | bytes 557088 | tf_op jit(solution)/shard_map/ppermute | solution.py:138
  406.2 25.3 %collective-permute-done.15 = f32[8,136,128]{2,1,0:T(8,128)} collective-permute-done((f32[8,136,128]{2,1,0:T(8,128)}, f32[8,136,128]{2,1,0:T(8,128)}, u32[]{:S(2)}, u32[]{:S(2)}) %collective-permute-start.15) | collective-permute-done | bytes 557088 | tf_op jit(solution)/shard_map/ppermute | solution.py:138
  434.9 17.6 %shard_map.96 = (bf16[512,1024]{1,0:T(8,128)(2,1)}, bf16[512,1024]{1,0:T(8,128)(2,1)}, bf16[512,1024]{1,0:T(8,128)(2,1)}) custom-call(bf16[512,1024]{1,0:T(8,128)(2,1)S(1)} %copy-done.4, bf16[512,1024]{1,0:T(8,128)(2,1)S(1)} %copy-done.7, bf16[512,1024]{1,0:T(8,128)(2,1)S(1)} %copy-done.10, f32[512,1024]{1,0:T(8,128)S(1)} %copy-done.14, ...), custom_call_target="tpu_custom_call" | custom-call | flops 5368709120 | bytes 4194304 | tf_op jit(solution)/shard_map/pallas_call | solution.py:259
  452.5 38.1 %all-gather.5.cloned.1.call-done = bf16[4096,1024]{1,0:T(8,128)(2,1)} async-done(((bf16[512,1024]{1,0:T(8,128)(2,1)}), bf16[4096,1024]{1,0:T(8,128)(2,1)}) %all-gather.5.cloned.1.call-update) | async-done | bytes 8388624 | tf_op jit(solution)/shard_map/all_gather | solution.py:241
  490.6 4.0 fusion.16
  498.7 5.1 add_add_fusion
  (108 shorter events, 44.0 us)
Async XLA Ops:
  7.2 308.2 %all-gather.3.cloned.1.call-start = ((), (), s32[]{:S(2)}) async-start(), calls=%async_computation | async-start | bytes 14155776 | tf_op jit(solution)/shard_map/all_gather | solution.py:191
  7.9 482.7 %all-gather.5.cloned.1.call-start = ((), (), s32[]{:S(2)}) async-start(), calls=%async_computation.1 | async-start | bytes 9437184 | tf_op jit(solution)/shard_map/all_gather | solution.py:241
  18.2 27.1 %collective-permute-start = (f32[8,136,128]{2,1,0:T(8,128)}, f32[8,136,128]{2,1,0:T(8,128)S(1)}, u32[]{:S(2)}, u32[]{:S(2)}) collective-permute-start(f32[8,136,128]{2,1,0:T(8,128)} %pad_maximum_fusion.1), channel_id=1, source_target_pairs={{0,4},{4,0},{8,12},{12,8},{16,20},{20,16},{24,28},{28,24},{1,5},{5... | collective-permute-start | bytes 1671176 | tf_op jit(solution)/shard_map/ppermute | solution.py:138
  45.7 29.4 %collective-permute-start.2 = (f32[8,136,128]{2,1,0:T(8,128)S(1)}, f32[8,136,128]{2,1,0:T(8,128)}, u32[]{:S(2)}, u32[]{:S(2)}) collective-permute-start(f32[8,136,128]{2,1,0:T(8,128)S(1)} %pad_maximum_fusion.2), channel_id=1, source_target_pairs={{0,16},{4,20},{8,24},{12,28},{1,17},{5,21},{9,25},{13,29},{2,18},{... | collective-permute-start | bytes 1671176 | tf_op jit(solution)/shard_map/ppermute | solution.py:138
  51.0 48.0 %collective-permute-start.1 = (f32[8,136,128]{2,1,0:T(8,128)S(1)}, f32[8,136,128]{2,1,0:T(8,128)}, u32[]{:S(2)}, u32[]{:S(2)}) collective-permute-start(f32[8,136,128]{2,1,0:T(8,128)S(1)} %pad_maximum_fusion.2), channel_id=1, source_target_pairs={{0,8},{4,12},{8,16},{12,20},{16,24},{20,28},{1,9},{5,13},{9,17},{1... | collective-permute-start | bytes 1671176 | tf_op jit(solution)/shard_map/ppermute | solution.py:138
  55.4 54.7 %collective-permute-start.3 = (f32[8,136,128]{2,1,0:T(8,128)S(1)}, f32[8,136,128]{2,1,0:T(8,128)}, u32[]{:S(2)}, u32[]{:S(2)}) collective-permute-start(f32[8,136,128]{2,1,0:T(8,128)S(1)} %pad_maximum_fusion.2), channel_id=1, source_target_pairs={{0,24},{4,28},{1,25},{5,29},{2,26},{6,30},{3,27},{7,31}} | collective-permute-start | bytes 1671176 | tf_op jit(solution)/shard_map/ppermute | solution.py:138
  111.7 190.3 %copy-start.11 = (f32[8,128,128]{2,1,0:T(8,128)}, f32[8,128,128]{2,1,0:T(8,128)S(1)}, u32[]{:S(2)}) copy-start(f32[8,128,128]{2,1,0:T(8,128)S(1)} %add_select_fusion.2.state_ref) | copy-start | bytes 1572868
  114.5 34.9 %collective-permute-start.7 = (bf16[512,768]{1,0:T(8,128)(2,1)}, bf16[512,768]{1,0:T(8,128)(2,1)}, u32[]{:S(2)}, u32[]{:S(2)}) collective-permute-start(bf16[512,768]{1,0:T(8,128)(2,1)} %get-tuple-element.47), channel_id=1, source_target_pairs={{0,0},{1,8},{2,16},{3,24},{4,4},{5,12},{6,20},{7,28},{8,1},{9,9},{... | collective-permute-start | bytes 2359304 | tf_op jit(solution)/shard_map/ppermute | solution.py:216
  121.9 30.0 %collective-permute-start.8 = (bf16[512,768]{1,0:T(8,128)(2,1)}, bf16[512,768]{1,0:T(8,128)(2,1)}, u32[]{:S(2)}, u32[]{:S(2)}) collective-permute-start(bf16[512,768]{1,0:T(8,128)(2,1)} %get-tuple-element.46), channel_id=1, source_target_pairs={{0,4},{1,12},{2,20},{3,28},{4,0},{5,8},{6,16},{7,24},{8,5},{9,13},... | collective-permute-start | bytes 2359304 | tf_op jit(solution)/shard_map/ppermute | solution.py:216
  123.3 160.2 %collective-permute-start.5 = (bf16[512,1536]{1,0:T(8,128)(2,1)}, bf16[512,1536]{1,0:T(8,128)(2,1)}, u32[]{:S(2)}, u32[]{:S(2)}) collective-permute-start(bf16[512,1536]{1,0:T(8,128)(2,1)} %param.11), channel_id=1, source_target_pairs={{0,2},{1,3},{2,0},{3,1},{4,6},{5,7},{6,4},{7,5},{8,10},{9,11},{10,... | collective-permute-start | bytes 4718600 | tf_op jit(solution)/shard_map/ppermute | solution.py:147
  149.3 152.7 %copy-start.2 = (bf16[512,1024]{1,0:T(8,128)(2,1)S(1)}, bf16[512,1024]{1,0:T(8,128)(2,1)}, u32[]{:S(2)}) copy-start(bf16[512,1024]{1,0:T(8,128)(2,1)} %q_ref.5) | copy-start | bytes 3145732
  149.3 152.7 %copy-start.6 = (bf16[512,1024]{1,0:T(8,128)(2,1)S(1)}, bf16[512,1024]{1,0:T(8,128)(2,1)}, u32[]{:S(2)}) copy-start(bf16[512,1024]{1,0:T(8,128)(2,1)} %k_ref.5) | copy-start | bytes 3145732
  149.3 152.7 %copy-start.9 = (bf16[512,1024]{1,0:T(8,128)(2,1)S(1)}, bf16[512,1024]{1,0:T(8,128)(2,1)}, u32[]{:S(2)}) copy-start(bf16[512,1024]{1,0:T(8,128)(2,1)} %v_ref.5) | copy-start | bytes 3145732
  153.2 158.1 %copy-start.15 = (bf16[2,512,768]{2,1,0:T(8,128)(2,1)}, bf16[2,512,768]{2,1,0:T(8,128)(2,1)S(1)}, u32[]{:S(2)}) copy-start(bf16[2,512,768]{2,1,0:T(8,128)(2,1)S(1)} %bitcast_dynamic-update-slice_fusion) | copy-start | bytes 4718596
  153.2 148.7 %collective-permute-start.10 = (bf16[1024,768]{1,0:T(8,128)(2,1)S(1)}, bf16[1024,768]{1,0:T(8,128)(2,1)S(1)}, u32[]{:S(2)}, u32[]{:S(2)}) collective-permute-start(bf16[1024,768]{1,0:T(8,128)(2,1)S(1)} %bitcast.31), channel_id=1, source_target_pairs={{0,2},{1,3},{2,0},{3,1},{4,6},{5,7},{6,4},{7,5},{8,10},{9,11},{10,... | collective-permute-start | bytes 4718600 | tf_op jit(solution)/shard_map/ppermute | solution.py:147
  283.5 29.0 %collective-permute-start.4 = (bf16[512,1536]{1,0:T(8,128)(2,1)}, bf16[512,1536]{1,0:T(8,128)(2,1)S(1)}, u32[]{:S(2)}, u32[]{:S(2)}) collective-permute-start(bf16[512,1536]{1,0:T(8,128)(2,1)} %param.11), channel_id=1, source_target_pairs={{0,1},{1,0},{2,3},{3,2},{4,5},{5,4},{6,7},{7,6},{8,9},{9,8},{10,11... | collective-permute-start | bytes 4718600 | tf_op jit(solution)/shard_map/ppermute | solution.py:151
  283.5 29.0 %collective-permute-start.6 = (bf16[512,1536]{1,0:T(8,128)(2,1)}, bf16[512,1536]{1,0:T(8,128)(2,1)S(1)}, u32[]{:S(2)}, u32[]{:S(2)}) collective-permute-start(bf16[512,1536]{1,0:T(8,128)(2,1)} %collective-permute-done.5), channel_id=1, source_target_pairs={{0,1},{1,0},{2,3},{3,2},{4,5},{5,4},{6,7},{7,6},{8,9},{9,8},{10,11... | collective-permute-start | bytes 4718600 | tf_op jit(solution)/shard_map/ppermute | solution.py:151
  284.0 28.5 %collective-permute-start.9 = (bf16[1024,768]{1,0:T(8,128)(2,1)S(1)}, bf16[1024,768]{1,0:T(8,128)(2,1)S(1)}, u32[]{:S(2)}, u32[]{:S(2)}) collective-permute-start(bf16[1024,768]{1,0:T(8,128)(2,1)S(1)} %bitcast.32), channel_id=1, source_target_pairs={{0,1},{1,0},{2,3},{3,2},{4,5},{5,4},{6,7},{7,6},{8,9},{9,8},{10,11... | collective-permute-start | bytes 4718600 | tf_op jit(solution)/shard_map/ppermute | solution.py:151
  301.9 13.5 %collective-permute-start.11 = (bf16[1024,768]{1,0:T(8,128)(2,1)S(1)}, bf16[1024,768]{1,0:T(8,128)(2,1)}, u32[]{:S(2)}, u32[]{:S(2)}) collective-permute-start(bf16[1024,768]{1,0:T(8,128)(2,1)S(1)} %collective-permute-done.10), channel_id=1, source_target_pairs={{0,1},{1,0},{2,3},{3,2},{4,5},{5,4},{6,7},{7,6},{8,9},{9,8},{10,11... | collective-permute-start | bytes 4718600 | tf_op jit(solution)/shard_map/ppermute | solution.py:151
  335.7 26.4 %collective-permute-start.12 = (f32[8,136,128]{2,1,0:T(8,128)S(1)}, f32[8,136,128]{2,1,0:T(8,128)}, u32[]{:S(2)}, u32[]{:S(2)}) collective-permute-start(f32[8,136,128]{2,1,0:T(8,128)S(1)} %pad_maximum_fusion), channel_id=1, source_target_pairs={{0,4},{4,0},{8,12},{12,8},{16,20},{20,16},{24,28},{28,24},{1,5},{5... | collective-permute-start | bytes 1671176 | tf_op jit(solution)/shard_map/ppermute | solution.py:138
  364.2 69.0 %copy-start.4 = (bf16[512,1024]{1,0:T(8,128)(2,1)S(1)}, bf16[512,1024]{1,0:T(8,128)(2,1)}, u32[]{:S(2)}) copy-start(bf16[512,1024]{1,0:T(8,128)(2,1)} %q_ref.5) | copy-start | bytes 3145732
  365.1 40.2 %collective-permute-start.14 = (f32[8,136,128]{2,1,0:T(8,128)}, f32[8,136,128]{2,1,0:T(8,128)}, u32[]{:S(2)}, u32[]{:S(2)}) collective-permute-start(f32[8,136,128]{2,1,0:T(8,128)} %pad_maximum_fusion.3), channel_id=1, source_target_pairs={{16,0},{20,4},{24,8},{28,12},{17,1},{21,5},{25,9},{29,13},{18,2},{... | collective-permute-start | bytes 1671176 | tf_op jit(solution)/shard_map/ppermute | solution.py:138
  366.4 38.9 %collective-permute-start.13 = (f32[8,136,128]{2,1,0:T(8,128)}, f32[8,136,128]{2,1,0:T(8,128)}, u32[]{:S(2)}, u32[]{:S(2)}) collective-permute-start(f32[8,136,128]{2,1,0:T(8,128)} %pad_maximum_fusion.3), channel_id=1, source_target_pairs={{8,0},{12,4},{16,8},{20,12},{24,16},{28,20},{9,1},{13,5},{17,9},{2... | collective-permute-start | bytes 1671176 | tf_op jit(solution)/shard_map/ppermute | solution.py:138
  367.7 63.8 %collective-permute-start.15 = (f32[8,136,128]{2,1,0:T(8,128)}, f32[8,136,128]{2,1,0:T(8,128)}, u32[]{:S(2)}, u32[]{:S(2)}) collective-permute-start(f32[8,136,128]{2,1,0:T(8,128)} %pad_maximum_fusion.3), channel_id=1, source_target_pairs={{24,0},{28,4},{25,1},{29,5},{26,2},{30,6},{27,3},{31,7}} | collective-permute-start | bytes 1671176 | tf_op jit(solution)/shard_map/ppermute | solution.py:138
  (20 other events, 280.6 us)
Sparse Core Ops, SparseCore 0:
  10.2 280.8 all-gather.2
  315.5 174.9 all-gather.4
